TPU v7x, 256 devices: a whole 4x4x8 slice. The times are simulated.
256 devices in a mesh: feat: 64 (over z, x, y_hi), pair: 4 (over y_lo, core).
Axes of the slice: x: 4, y: 4 (y_hi: 2, y_lo: 2; y = y_hi * 2 + y_lo), z: 8, core: 2. Of those that a mesh axis runs over, the one named last changes fastest.
Arguments:
- resid: bfloat16 [4, 1024, 2048], P('pair'), may hold values from -6 to 6
- enc_weight: bfloat16 [4, 2048, 16384], P('pair', None, 'feat'), may hold values from -0.125 to 0.125
- enc_bias: float32 [4, 16384], P('pair', 'feat'), may hold values from -3 to 3
- active: int32 [4, 1024, 64], P('pair'), may hold values from 0 to 16383, all different within a row
- dec_weight: bfloat16 [4, 4, 16384, 2048], P('pair', None, 'feat'), may hold values from -0.75 to 0.75
- dec_bias: float32 [4, 2048], P('pair'), may hold values from -3 to 3
- target: bfloat16 [4, 1024, 2048], P('pair', 'feat'), may hold values from -6 to 6
Outputs:
- error: float32 [4, 1024, 2048], P('pair', 'feat')
- dec_grad: bfloat16 [4, 4, 16384, 2048], P('pair', None, 'feat')
Inputs may be any that keep to these rules, and one draw needn't show every extreme that they name: `active`: within one layer, the 64 indices of a token are distinct; every feature number occurs somewhere in the array.
All inputs are finite; a program needn't handle non-finite values.
Results may differ from a plain program's by a relative error of at most 0.0058.
Values may be sent and summed in bfloat16 or wider, within the bound.
A program may use at most 128 MiB of HBM per device.

v0:
```python
import jax
import jax.numpy as jnp
from jax import lax
from jax.sharding import PartitionSpec as P


def local(resid, enc_weight, enc_bias, active, dec_weight, dec_bias, target):
    slice_width = enc_weight.shape[2]
    model_width = resid.shape[2]
    layers = dec_weight.shape[1]
    shard_rows = target.shape[1]
    feat_index = lax.axis_index("feat")
    pair_index = lax.axis_index("pair")
    columns = feat_index * slice_width + jnp.arange(slice_width, dtype=jnp.int32)
    chosen = jnp.any(active[0][:, :, None] == columns[None, None, :], axis=1)
    pre_act = (
        jnp.dot(resid[0], enc_weight[0], preferred_element_type=jnp.float32) + enc_bias[0][None, :]
    )
    values = jnp.where(chosen, jnp.maximum(pre_act, 0.0), 0.0).astype(jnp.bfloat16)
    gathered = lax.all_gather(values[None], "pair", axis=0, tiled=True)
    decoders = dec_weight[0]

    def add_source(source, partial_value):
        left_rows = lax.dynamic_index_in_dim(gathered, source, 0, keepdims=False)
        weight_rows = lax.dynamic_index_in_dim(decoders, source, 0, keepdims=False)
        return partial_value + jnp.dot(left_rows, weight_rows, preferred_element_type=jnp.float32)

    rebuilt = lax.psum_scatter(
        lax.fori_loop(
            0,
            pair_index + 1,
            add_source,
            jnp.zeros((shard_rows * lax.axis_size("feat"), model_width), jnp.float32),
        ),
        "feat",
        scatter_dimension=0,
        tiled=True,
    )
    error_shard = rebuilt + dec_bias[0][None, :] - target[0].astype(jnp.float32)
    error_half = lax.all_gather(error_shard.astype(jnp.bfloat16), "feat", axis=0, tiled=True)

    def source_grad(source, error_rows):
        left_rows = lax.dynamic_index_in_dim(gathered, source, 0, keepdims=False)
        product = lax.dot_general(
            left_rows, error_rows, (((0,), (0,)), ((), ())), preferred_element_type=jnp.float32
        )
        return product.astype(jnp.bfloat16)

    def add_grad(source, gradients):
        return lax.dynamic_update_index_in_dim(
            gradients, source_grad(source, error_half), source, 0
        )

    empty = jnp.zeros((layers, slice_width, model_width), jnp.bfloat16)
    gradients = lax.fori_loop(0, pair_index + 1, add_grad, empty)
    return (error_shard[None], gradients[None])


def solution(mesh):
    in_specs = (
        P("pair", None, None),
        P("pair", None, "feat"),
        P("pair", "feat"),
        P("pair", None, None),
        P("pair", None, "feat", None),
        P("pair", None),
        P("pair", "feat", None),
    )
    out_specs = (P("pair", "feat", None), P("pair", None, "feat", None))
    return jax.shard_map(local, mesh=mesh, in_specs=in_specs, out_specs=out_specs, check_vma=False)
```

profile of v0, /device:TPU:8, one launch (start us, length us, event | category | flops | bytes accessed | tf_op | source)
XLA Modules:
  0.0 627.2 jit_solution(8252635476921312662)
XLA Ops:
  7.2 0.0 copy-start
  7.2 0.0 all-gather.6.cloned.1.call-start
  7.2 1.2 copy.10
  8.5 11.5 %compare_reduce_fusion = pred[1024,256]{1,0:T(8,128)(4,1)S(1)} fusion(s32[256]{0:T(256)S(1)} %iota_add_fusion, s32[1024,64]{1,0:T(8,128)S(1)} %copy.10), kind=kLoop, calls=%fused_computation.12 | loop fusion | flops 33292288 | bytes 525312 | tf_op jit(solution)/shard_map/reduce_or | solution.py:15
  19.9 0.0 copy-done
  20.0 4.2 fusion.21
  24.2 0.0 all-gather.6.cloned.1.call-update
  24.2 0.0 reduce-scatter.2.cloned.1.call-start
  24.3 32.9 %all-gather.6.cloned.1.call-done = bf16[4096,256]{1,0:T(8,128)(2,1)} async-done(((bf16[1024,256]{1,0:T(8,128)(2,1)}), bf16[4096,256]{1,0:T(8,128)(2,1)}) %all-gather.6.cloned.1.call-update) | async-done | bytes 2097168 | tf_op jit(solution)/shard_map/all_gather | solution.py:20
  57.2 0.0 copy-start.1
  57.2 4.3 broadcast_in_dim.22
  61.5 0.0 copy-done.1
  61.5 24.6 %while.20 = (s32[]{:T(128)}, f32[1024,2048]{1,0:T(8,128)}, s32[]{:T(128)}, bf16[4,1024,256]{2,1,0:T(8,128)(2,1)S(1)}, bf16[4,256,2048]{2,1,0:T(8,128)(2,1)}, /*index=5*/s32[]{:T(128)}, s32[]{:T(128)}, s32[]{:T(128)}) while((s32[]{:T(128)}, f32[1024,2048]{1,0:T(8,128)}, s32[]{:T(128)}, bf16[4,1024,256]{2,1,0:T(8,128)(2,1)S(1)}, ...), condition=%wide.region_2.3_spmd, body=%wide.region_1.2_spmd.sunk | while | flops 1075838976 | bytes 18351224 | solution.py:29
  61.5 8.2 %convolution_add_fusion.2 = f32[1024,2048]{1,0:T(8,128)} fusion(f32[1024,2048]{1,0:T(8,128)} %get-tuple-element.155, bf16[4,256,2048]{2,1,0:T(8,128)(2,1)} %get-tuple-element.166, s32[]{:T(128)S(6)} %select_n.21, bf16[4,1024,256]{2,1,0:T(8,128)(2,1)S(1)} %get-tuple-element.165), kind=kOutput, calls=%fused_computation.clone.1 | convolution fusion | flops 1075838976 | bytes 18351104 | tf_op jit(solution)/shard_map/while/body/dot_general | solution.py:26
  69.7 8.2 %convolution_add_fusion.2 = f32[1024,2048]{1,0:T(8,128)} fusion(f32[1024,2048]{1,0:T(8,128)} %get-tuple-element.155, bf16[4,256,2048]{2,1,0:T(8,128)(2,1)} %get-tuple-element.166, s32[]{:T(128)S(6)} %select_n.21, bf16[4,1024,256]{2,1,0:T(8,128)(2,1)S(1)} %get-tuple-element.165), kind=kOutput, calls=%fused_computation.clone.1 | convolution fusion | flops 1075838976 | bytes 18351104 | tf_op jit(solution)/shard_map/while/body/dot_general | solution.py:26
  77.9 8.2 %convolution_add_fusion.2 = f32[1024,2048]{1,0:T(8,128)} fusion(f32[1024,2048]{1,0:T(8,128)} %get-tuple-element.155, bf16[4,256,2048]{2,1,0:T(8,128)(2,1)} %get-tuple-element.166, s32[]{:T(128)S(6)} %select_n.21, bf16[4,1024,256]{2,1,0:T(8,128)(2,1)S(1)} %get-tuple-element.165), kind=kOutput, calls=%fused_computation.clone.1 | convolution fusion | flops 1075838976 | bytes 18351104 | tf_op jit(solution)/shard_map/while/body/dot_general | solution.py:26
  86.1 0.0 copy-start.2
  86.1 0.0 copy-start.3
  86.1 0.0 reduce-scatter.2.cloned.1.call-update
  86.1 0.0 all-gather.4.cloned.1.call-start
  86.2 393.7 %reduce-scatter.2.cloned.1.call-done = f32[16,2048]{1,0:T(8,128)} async-done(((f32[1024,2048]{1,0:T(8,128)}), f32[16,2048]{1,0:T(8,128)}) %reduce-scatter.2.cloned.1.call-update) | async-done | bytes 131088 | tf_op jit(solution)/shard_map/reduce_scatter | solution.py:28
  479.8 0.0 copy-done.2
  479.8 0.0 copy-done.3
  479.8 1.6 fusion.25
  481.4 0.0 all-gather.4.cloned.1.call-update
  481.4 123.4 %all-gather.4.cloned.1.call-done = bf16[1024,2048]{1,0:T(8,128)(2,1)} async-done(((bf16[16,2048]{1,0:T(8,128)(2,1)}), bf16[1024,2048]{1,0:T(8,128)(2,1)}) %all-gather.4.cloned.1.call-update) | async-done | bytes 4194320 | tf_op jit(solution)/shard_map/all_gather | solution.py:40
  604.8 2.5 broadcast_in_dim.25
  607.4 13.3 %while.21 = (s32[]{:T(128)}, bf16[4,256,2048]{2,1,0:T(8,128)(2,1)}, s32[]{:T(128)}, bf16[4,1024,256]{2,1,0:T(8,128)(2,1)S(1)}, bf16[1024,2048]{1,0:T(8,128)(2,1)}, /*index=5*/s32[]{:T(128)}, s32[]{:T(128)}, s32[]{:T(128)}) while((s32[]{:T(128)}, bf16[4,256,2048]{2,1,0:T(8,128)(2,1)}, s32[]{:T(128)}, bf16[4,1024,256]{2,1,0:T(8,128)(2,1)S(1)}, ...), condition=%wide.region_5.6_spmd, body=%wide.region_4.5_spmd.sunk | while | flops 1074266112 | bytes 5768311 | solution.py:55
  607.4 4.4 fusion.37
  611.8 4.4 fusion.37
  616.2 4.4 fusion.37
  (1 shorter events, 0.0 us)
Async XLA Ops:
  7.2 12.8 %copy-start = (bf16[1,2048,256]{2,1,0:T(8,128)(2,1)S(1)}, bf16[1,2048,256]{2,1,0:T(8,128)(2,1)}, u32[]{:S(2)}) copy-start(bf16[1,2048,256]{2,1,0:T(8,128)(2,1)} %param.12) | copy-start | bytes 3145732
  7.2 50.0 %all-gather.6.cloned.1.call-start = ((), (), s32[]{:S(2)}) async-start(), calls=%async_computation.3 | async-start | bytes 2621440 | tf_op jit(solution)/shard_map/all_gather | solution.py:20
  24.2 455.6 %reduce-scatter.2.cloned.1.call-start = ((), (), s32[]{:S(2)}) async-start(), calls=%async_computation.1 | async-start | bytes 8519680 | tf_op jit(solution)/shard_map/reduce_scatter | solution.py:28
  57.2 4.3 copy-start.1
  86.1 393.7 %copy-start.2 = (bf16[1,16,2048]{2,1,0:T(8,128)(2,1)S(1)}, bf16[1,16,2048]{2,1,0:T(8,128)(2,1)}, u32[]{:S(2)}) copy-start(bf16[1,16,2048]{2,1,0:T(8,128)(2,1)} %param.17) | copy-start | bytes 196612
  86.1 393.7 %copy-start.3 = (f32[1,2048]{1,0:T(1,128)S(1)}, f32[1,2048]{1,0:T(1,128)}, u32[]{:S(2)}) copy-start(f32[1,2048]{1,0:T(1,128)} %param.16) | copy-start | bytes 24580
  86.1 518.7 %all-gather.4.cloned.1.call-start = ((), (), s32[]{:S(2)}) async-start(), calls=%async_computation.2 | async-start | bytes 4259840 | tf_op jit(solution)/shard_map/all_gather | solution.py:40
Sparse Core Ops, SparseCore 0:
  24.3 32.7 all-gather.5
  86.2 393.5 reduce-scatter.1
  483.9 120.9 all-gather.3
where the time goes:
time: 628 us; the launch traced here: 627 us
  waiting for transfers between devices  550 us (88%)
  matrix products  42.1 us (7%)
  between operations  13.8 us (2%)
  other arithmetic  13.1 us (2%)
  local copies, waits for them, and re-layouts  8.05 us (1%)
    reduce_scatter x1, waiting for transfers between devices, local(): lax.psum_scatter(lax.fori_loop(0, pair_index + 1, add_source, jnp.zeros((...  394 us
    all_gather x1, waiting for transfers between devices, local(): lax.all_gather(error_shard.astype(jnp.bfloat16), 'feat', axis=0, tiled=True)  123 us
    all_gather x1, waiting for transfers between devices, local(): gathered = lax.all_gather(values[None], 'pair', axis=0, tiled=True)  32.9 us
    dot_general x3, matrix products, add_source(): jnp.dot(left_rows, weight_rows, preferred_element_type=jnp.float32)  24.6 us
    dot_general x3, matrix products, source_grad(): lax.dot_general(left_rows, error_rows, (((0,), (0,)), ((), ())), preferre...  13.3 us
  transfers between devices with their start and end apart: 3, of which 3 were waited for; matrix products, arithmetic and copies ran while one was open for 0% of the time, Pallas kernels for 0%

commit v1 on v0

v1 whole, which is shorter than its diff:
```python
import jax
import jax.numpy as jnp
from jax import lax
from jax.experimental import pallas as pl
from jax.experimental.pallas import tpu as pltpu
from jax.sharding import PartitionSpec as P

MESH = pl.DeviceIdType.MESH
F32, BF16 = jnp.float32, jnp.bfloat16
NZ, NX, NY = 8, 4, 2
UP, DN = 0, 1


def values_kernel(active_ref, resid_ref, enc_ref, bias_ref, out_ref):
    width = enc_ref.shape[1]
    rows = resid_ref.shape[0]
    base = lax.axis_index("feat") * width
    local = active_ref[...].T - base
    word = lax.shift_right_arithmetic(local, 5)
    bit = lax.shift_left(jnp.int32(1), local & 31)
    words = [
        jnp.sum(jnp.where(word == w, bit, 0), axis=0, keepdims=True) for w in range(width // 32)
    ]
    spread = jnp.concatenate([jnp.broadcast_to(w, (32, rows)) for w in words], axis=0)
    place = lax.broadcasted_iota(jnp.int32, (width, rows), 0) & 31
    chosen = (lax.shift_right_logical(spread, place) & 1).astype(F32).T
    pre = jnp.dot(resid_ref[...], enc_ref[...], preferred_element_type=F32) + bias_ref[...]
    out_ref[...] = jnp.where(chosen > 0.5, jnp.maximum(pre, 0.0), 0.0).astype(BF16)


def values_of(active, resid, enc, bias):
    tokens, model = resid.shape
    width = enc.shape[1]
    block = 256
    return pl.pallas_call(
        values_kernel,
        grid=(tokens // block,),
        out_shape=jax.ShapeDtypeStruct((tokens, width), BF16),
        in_specs=[
            pl.BlockSpec((block, active.shape[1]), lambda i: (i, 0)),
            pl.BlockSpec((block, model), lambda i: (i, 0)),
            pl.BlockSpec((model, width), lambda i: (0, 0)),
            pl.BlockSpec((1, width), lambda i: (0, 0)),
        ],
        out_specs=pl.BlockSpec((block, width), lambda i: (i, 0)),
    )(active, resid, enc, bias)


def grad_kernel(cat_ref, err_ref, out_ref, turned):
    @pl.when(pl.program_id(0) == 0)
    def _():
        turned[...] = cat_ref[...].T

    layers, width, cols = out_ref.shape
    product = jnp.dot(turned[...], err_ref[...], preferred_element_type=F32)
    out_ref[...] = product.astype(BF16).reshape(layers, width, cols)


def grads_of(cat, err, layers):
    tokens, stacked = cat.shape
    model = err.shape[1]
    block = 256
    return pl.pallas_call(
        grad_kernel,
        grid=(model // block,),
        out_shape=jax.ShapeDtypeStruct((layers, stacked // layers, model), BF16),
        in_specs=[
            pl.BlockSpec((tokens, stacked), lambda i: (0, 0)),
            pl.BlockSpec((tokens, block), lambda i: (0, i)),
        ],
        out_specs=pl.BlockSpec((layers, stacked // layers, block), lambda i: (0, 0, i)),
        scratch_shapes=[pltpu.VMEM((stacked, tokens), BF16)],
    )(cat, err)


class Ring:
    def __init__(self, size, index, device, sends, recvs):
        self.size, self.index, self.device = size, index, device
        self.sends, self.recvs = sends, recvs
        self.far = size // 2
        self.started = []

    def at(self, offset):
        return lax.rem(self.index + offset + self.size, self.size)

    def copy(self, way, half, step, src, dst):
        toward = self.at(1 if way == UP else -1)
        return pltpu.make_async_remote_copy(
            src_ref=src,
            dst_ref=dst,
            send_sem=self.sends.at[way, half, step - 1],
            recv_sem=self.recvs.at[way, half, step - 1],
            device_id=self.device(toward),
            device_id_type=MESH,
        )

    def go(self, *what):
        copy = self.copy(*what)
        copy.start()
        self.started.append(copy)

    def drain(self):
        for copy in self.started:
            copy.wait_send()

    def reach(self, way, half):
        return self.far if way == half else self.far - 1


STREAMS = ((UP, 0), (DN, 1), (UP, 1), (DN, 0))


class Reduce(Ring):
    def __init__(self, size, index, device, sends, recvs, own, held):
        super().__init__(size, index, device, sends, recvs)
        self.own, self.held = own, held

    def slot(self, way, half, step):
        return self.held.at[way, half, step - 1]

    def first(self):
        for way, half in STREAMS:
            far = self.reach(way, half)
            dest = self.at(far if way == UP else -far)
            self.go(way, half, far, self.own(dest, half), self.slot(way, half, far))

    def arrive(self, way, half, step):
        slot = self.slot(way, half, step)
        self.copy(way, half, step, slot, slot).wait_recv()
        return slot

    def pass_on(self, way, half, step):
        slot = self.arrive(way, half, step + 1)
        dest = self.at(step if way == UP else -step)
        own = self.own(dest, half)
        slot[...] = (slot[...].astype(F32) + own[...].astype(F32)).astype(BF16)
        self.go(way, half, step, slot, self.slot(way, half, step))

    def total(self, half):
        up = self.arrive(UP, half, 1)
        down = self.arrive(DN, half, 1)
        own = self.own(self.index, half)
        return own[...].astype(F32) + (up[...].astype(F32) + down[...].astype(F32))


class Gather(Ring):
    def __init__(self, size, index, device, sends, recvs, view):
        super().__init__(size, index, device, sends, recvs)
        self.view = view

    def first(self):
        for way, half in STREAMS:
            block = self.view(self.index, half)
            self.go(way, half, 1, block, block)

    def arrive(self, way, half, step):
        block = self.view(self.at(-step if way == UP else step), half)
        self.copy(way, half, step, block, block).wait_recv()
        return block

    def pass_on(self, way, half, step):
        if step <= self.reach(way, half):
            block = self.arrive(way, half, step - 1)
            self.go(way, half, step, block, block)

    def last(self):
        for way, half in STREAMS:
            self.arrive(way, half, self.reach(way, half))


def exchange_kernel(
    vals_ref, dec_ref, bias_ref, target_ref,
    err_ref, full_ref, cat_ref,
    part, mid_a, mid_b, end_a, end_b,
    held_az, held_ax, held_bx, held_bz, held_y, last_y,
    pair_send, pair_recv,
    s_az, r_az, s_ax, r_ax, s_bx, r_bx, s_bz, r_bz,
    g_ax, h_ax, g_az, h_az, g_bz, h_bz, g_bx, h_bx,
    y_send, y_recv,
):
    feat, pair = lax.axis_index("feat"), lax.axis_index("pair")
    z, x, y = feat // (NX * NY), lax.rem(feat // NY, NX), lax.rem(feat, NY)
    width = vals_ref.shape[2]
    cut = part.shape[2] // 2
    cols_a, cols_b = pl.ds(0, cut), pl.ds(cut, cut)

    def spot(zz, xx, yy):
        return ((zz * NX + xx) * NY + yy, pair)

    along_z = lambda other: spot(other, x, y)
    along_x = lambda other: spot(z, other, y)
    across = spot(z, x, 1 - y)
    core_mate = (feat, pair + 1 - 2 * lax.rem(pair, 2))
    chip_mate = (feat, lax.rem(pair + 2, 4))

    barrier = pltpu.get_barrier_semaphore()
    greeted = (
        along_z(lax.rem(z + 1, NZ)), along_z(lax.rem(z + NZ - 1, NZ)),
        along_x(lax.rem(x + 1, NX)), along_x(lax.rem(x + NX - 1, NX)),
        across, core_mate, chip_mate,
    )
    for device in greeted:
        pl.semaphore_signal(barrier, inc=1, device_id=device, device_id_type=MESH)
    pl.semaphore_wait(barrier, len(greeted))

    pieces = pair_recv.shape[1]
    span = NZ // pieces

    def column(slot):
        return pl.ds(pl.multiple_of(slot * width, width), width)

    def piece(ref, slot, c):
        return ref.at[pl.ds(c * span, span), :, column(slot)]

    def send_piece(kind, src, slot, c, device):
        return pltpu.make_async_remote_copy(
            src_ref=src, dst_ref=piece(cat_ref, slot, c),
            send_sem=pair_send.at[kind, c], recv_sem=pair_recv.at[slot, c],
            device_id=device, device_id_type=MESH,
        )

    def await_piece(slot, c):
        block = piece(cat_ref, slot, c)
        send_piece(0, block, slot, c, core_mate).wait_recv()

    mine = lambda c: vals_ref.at[pl.ds(c * span, span)]
    low_chip, low_core = pair < 2, lax.rem(pair, 2) == 0
    relayed = lax.rem(pair, 2)

    @pl.when(low_chip)
    def _():
        for c in range(pieces):
            send_piece(0, mine(c), pair, c, chip_mate).start()

    @pl.when(low_core)
    def _():
        for c in range(pieces):
            send_piece(1, mine(c), pair, c, core_mate).start()

    for slot in range(4):

        @pl.when(pair == slot)
        def _():
            cat_ref[:, :, slot * width : (slot + 1) * width] = vals_ref[...]

        @pl.when(pair < slot)
        def _():
            cat_ref[:, :, slot * width : (slot + 1) * width] = jnp.zeros(
                (NZ, vals_ref.shape[1], width), BF16
            )

    @pl.when(jnp.logical_not(low_chip))
    def _():
        for c in range(pieces):
            await_piece(relayed, c)
            send_piece(2, piece(cat_ref, relayed, c), relayed, c, core_mate).start()
        for c in range(pieces):
            await_piece(1 - relayed, c)

    @pl.when(pair == 1)
    def _():
        for c in range(pieces):
            await_piece(0, c)

    @pl.when(pair == 3)
    def _():
        for c in range(pieces):
            await_piece(2, c)

    step = 256

    @pl.loop(0, part.shape[2] // step)
    def _(i):
        cols = pl.ds(pl.multiple_of(i * step, step), step)
        rows = cat_ref[...].reshape(-1, cat_ref.shape[2])
        product = jnp.dot(rows, dec_ref[:, cols], preferred_element_type=F32)
        part[:, :, cols] = product.astype(BF16).reshape(NZ, -1, step)

    def rows32(index, half):
        return pl.ds(pl.multiple_of(index * 32 + half * 16, 16), 16)

    az = Reduce(NZ, z, along_z, s_az, r_az, lambda i, h: part.at[i, pl.ds(h * 64, 64), cols_a], held_az)
    bx = Reduce(
        NX, x, along_x, s_bx, r_bx,
        lambda i, h: part.at[pl.ds(h * 4, 4), pl.ds(pl.multiple_of(i * 32, 32), 32), cols_b], held_bx,
    )
    ax = Reduce(NX, x, along_x, s_ax, r_ax, lambda i, h: mid_a.at[rows32(i, h)], held_ax)
    bz = Reduce(NZ, z, along_z, s_bz, r_bz, lambda i, h: mid_b.at[i, pl.ds(h * 16, 16)], held_bz)
    az.first()
    bx.first()
    az.pass_on(UP, 0, 3)
    az.pass_on(DN, 1, 3)
    az.pass_on(UP, 1, 2)
    az.pass_on(DN, 0, 2)
    bx.pass_on(UP, 0, 1)
    bx.pass_on(DN, 1, 1)
    az.pass_on(UP, 0, 2)
    az.pass_on(DN, 1, 2)
    az.pass_on(UP, 1, 1)
    az.pass_on(DN, 0, 1)
    az.pass_on(UP, 0, 1)
    az.pass_on(DN, 1, 1)
    for half in range(2):
        mid_b[half * 4 : half * 4 + 4] = bx.total(half).astype(BF16)
    bz.first()
    for half in range(2):
        mid_a[half * 64 : half * 64 + 64] = az.total(half).astype(BF16)
    ax.first()
    for way, half in ((UP, 0), (DN, 1)):
        bz.pass_on(way, half, 3)
    for way, half in ((UP, 1), (DN, 0)):
        bz.pass_on(way, half, 2)
    for way, half in ((UP, 0), (DN, 1)):
        ax.pass_on(way, half, 1)
    for way, half in ((UP, 0), (DN, 1)):
        bz.pass_on(way, half, 2)
    for way, half in ((UP, 1), (DN, 0)):
        bz.pass_on(way, half, 1)
    for way, half in ((UP, 0), (DN, 1)):
        bz.pass_on(way, half, 1)

    def over_y(which, src, dst):
        return pltpu.make_async_remote_copy(
            src_ref=src, dst_ref=dst, send_sem=y_send.at[which], recv_sem=y_recv.at[which],
            device_id=across, device_id_type=MESH,
        )

    for half in range(2):
        end_a[half] = ax.total(half)
        held_y[0, half] = end_a[half].astype(BF16)
    copy_a = over_y(0, held_y.at[0, 1 - y], last_y.at[0])
    copy_a.start()
    for half in range(2):
        end_b[half] = bz.total(half)
        held_y[1, half] = end_b[half].astype(BF16)
    copy_b = over_y(1, held_y.at[1, 1 - y], last_y.at[1])
    copy_b.start()

    my_rows = pl.ds(pl.multiple_of(x * 32 + y * 16, 16), 16)
    for which, copy, end in ((0, copy_a, end_a), (1, copy_b, end_b)):
        copy.wait_recv()
        cols = slice(which * cut, which * cut + cut)
        rebuilt = end[y] + last_y[which].astype(F32)
        error = rebuilt + bias_ref[:, cols] - target_ref[:, cols].astype(F32)
        err_ref[:, cols] = error
        full_ref[z, my_rows, cols] = error.astype(BF16)

    own_block = full_ref.at[z, my_rows]
    other_block = full_ref.at[z, pl.ds(pl.multiple_of(x * 32 + (1 - y) * 16, 16), 16)]
    copy_e = over_y(2, own_block, own_block)
    copy_e.start()
    over_y(2, other_block, other_block).wait_recv()
    gax = Gather(NX, x, along_x, g_ax, h_ax, lambda i, h: full_ref.at[z, rows32(i, h), cols_a])
    gbz = Gather(NZ, z, along_z, g_bz, h_bz, lambda i, h: full_ref.at[i, rows32(x, h), cols_b])
    gaz = Gather(NZ, z, along_z, g_az, h_az, lambda i, h: full_ref.at[i, pl.ds(h * 64, 64), cols_a])
    gbx = Gather(
        NX, x, along_x, g_bx, h_bx,
        lambda i, h: full_ref.at[pl.ds(h * 4, 4), pl.ds(pl.multiple_of(i * 32, 32), 32), cols_b],
    )
    gax.first()
    gbz.first()
    for way, half in STREAMS:
        gax.pass_on(way, half, 2)
    for way, half in STREAMS:
        gbz.pass_on(way, half, 2)
    gax.last()
    gaz.first()
    for way, half in STREAMS:
        gbz.pass_on(way, half, 3)
    for way, half in STREAMS:
        gbz.pass_on(way, half, 4)
    gbz.last()
    gbx.first()
    for way, half in STREAMS:
        gaz.pass_on(way, half, 2)
    for way, half in STREAMS:
        gbx.pass_on(way, half, 2)
    for way, half in STREAMS:
        gaz.pass_on(way, half, 3)
    for way, half in STREAMS:
        gaz.pass_on(way, half, 4)
    gbx.last()
    gaz.last()

    for ring in (az, bx, ax, bz, gax, gbz, gaz, gbx):
        ring.drain()
    for copy in (copy_a, copy_b, copy_e):
        copy.wait_send()

    @pl.when(low_chip)
    def _():
        for c in range(pieces):
            send_piece(0, mine(c), pair, c, chip_mate).wait_send()

    @pl.when(low_core)
    def _():
        for c in range(pieces):
            send_piece(1, mine(c), pair, c, core_mate).wait_send()

    @pl.when(jnp.logical_not(low_chip))
    def _():
        for c in range(pieces):
            send_piece(2, piece(cat_ref, relayed, c), relayed, c, core_mate).wait_send()


def exchange(vals, dec, bias, target):
    tokens, width = vals.shape
    stacked, model = dec.shape
    cut = model // 2
    pieces = 4
    dma = pltpu.SemaphoreType.DMA
    vmem = pl.BlockSpec(memory_space=pltpu.VMEM)
    block = tokens // NZ
    long, short = dma((2, 2, NZ // 2)), dma((2, 2, NX // 2))
    return pl.pallas_call(
        exchange_kernel,
        out_shape=(
            jax.ShapeDtypeStruct(target.shape, F32),
            jax.ShapeDtypeStruct((NZ, block, model), BF16),
            jax.ShapeDtypeStruct((NZ, block, stacked), BF16),
        ),
        in_specs=[vmem] * 4,
        out_specs=(vmem,) * 3,
        scratch_shapes=[
            pltpu.VMEM((NZ, block, model), BF16),
            pltpu.VMEM((block, cut), BF16),
            pltpu.VMEM((NZ, 32, cut), BF16),
            pltpu.VMEM((2, 16, cut), F32),
            pltpu.VMEM((2, 16, cut), F32),
            pltpu.VMEM((2, 2, NZ // 2, 64, cut), BF16),
            pltpu.VMEM((2, 2, NX // 2, 16, cut), BF16),
            pltpu.VMEM((2, 2, NX // 2, 4, 32, cut), BF16),
            pltpu.VMEM((2, 2, NZ // 2, 16, cut), BF16),
            pltpu.VMEM((2, 2, 16, cut), BF16),
            pltpu.VMEM((2, 16, cut), BF16),
            dma((3, pieces)),
            dma((4, pieces)),
            long, long, short, short, short, short, long, long,
            short, short, long, long, long, long, short, short,
            dma((3,)),
            dma((3,)),
        ],
        compiler_params=pltpu.CompilerParams(
            collective_id=0, has_side_effects=True, vmem_limit_bytes=60 * 1024 * 1024
        ),
    )(vals.reshape(NZ, block, width), dec, bias, target)


def local(resid, enc_weight, enc_bias, active, dec_weight, dec_bias, target):
    layers, width, model = dec_weight.shape[1:]
    tokens = resid.shape[1]
    vals = values_of(active[0], resid[0], enc_weight[0], enc_bias)
    error, full, cat = exchange(
        vals, dec_weight[0].reshape(layers * width, model), dec_bias, target[0]
    )
    grads = grads_of(cat.reshape(tokens, -1), full.reshape(tokens, model), layers)
    return error[None], grads[None]


def solution(mesh):
    in_specs = (
        P("pair", None, None),
        P("pair", None, "feat"),
        P("pair", "feat"),
        P("pair", None, None),
        P("pair", None, "feat", None),
        P("pair", None),
        P("pair", "feat", None),
    )
    out_specs = (P("pair", "feat", None), P("pair", None, "feat", None))
    return jax.shard_map(local, mesh=mesh, in_specs=in_specs, out_specs=out_specs, check_vma=False)
```

time: 628 us -> 127 us (0.20)
  waiting for transfers between devices: 550 us -> 0 us
  Pallas kernels: 0 us -> 123 us
  matrix products: 42.1 us -> 0 us
  between operations: 13.8 us -> 0.65 us
  other arithmetic: 13.1 us -> 0 us
    reduce_scatter x1 -> x0, waiting for transfers between devices: 394 us -> none  [local(): lax.psum_scatter(lax.fori_loop(0, pair_index + 1, add_source, jnp.zeros((...]
    all_gather x2 -> x0, waiting for transfers between devices: 156 us -> none  [the longest x1 123 us: local(): lax.all_gather(error_shard.astype(jnp.bfloat16), 'feat', axis=0, tiled=True)]
    pallas_call x0 -> x3, Pallas kernels: none -> 123 us  [the longest x1 107 us: exchange(): pl.pallas_call(exchange_kernel, out_shape=(jax.ShapeDtypeStruct(target.sh...]
    dot_general x7 -> x0, matrix products: 42.1 us -> none  [the longest x3 24.6 us: add_source(): jnp.dot(left_rows, weight_rows, preferred_element_type=jnp.float32)]
    reduce_or x1 -> x0, other arithmetic: 11.5 us -> none  [local(): chosen = jnp.any(active[0][:, :, None] == columns[None, None, :], axis=1)]
    broadcast_in_dim x2 -> x0, local copies, waits for them, and re-layouts: 6.81 us -> none  [the longest x1 4.28 us: local(): jnp.zeros((shard_rows * lax.axis_size('feat'), model_width), jnp.float32)]
  transfers between devices with their start and end apart: 3 -> 0, of which waited for: 3 -> 0; matrix products, arithmetic and copies ran while one was open for 0% -> 0% of each run, Pallas kernels for 0% -> 0%
where the time goes in v1:
time: 127 us
  Pallas kernels  123 us (97%)
  local copies, waits for them, and re-layouts  2.61 us (2%)
    pallas_call x1, Pallas kernels, exchange(): pl.pallas_call(exchange_kernel, out_shape=(jax.ShapeDtypeStruct(target.sh...  107 us
    pallas_call x1, Pallas kernels, grads_of(): pl.pallas_call(grad_kernel, grid=(model // block,), out_shape=jax.ShapeDt...  10.7 us
    pallas_call x1, Pallas kernels, values_of(): pl.pallas_call(values_kernel, grid=(tokens // block,), out_shape=jax.Shap...  5.19 us
    unnamed x4, local copies, waits for them, and re-layouts  2.61 us

profile of v1, /device:TPU:8, one launch (start us, length us, event | category | flops | bytes accessed | tf_op | source)
XLA Modules:
  0.0 126.6 jit_solution(6165027533316193081)
XLA Ops:
  0.6 1.9 %copy.9 = s32[1,1024,64]{2,1,0:T(8,128)} copy(s32[1,1024,64]{1,2,0:T(8,128)} %param.10) | data formatting | bytes 524288 | tf_op args[3]
  2.6 5.2 %shard_map.86 = bf16[1024,256]{1,0:T(8,128)(2,1)} custom-call(s32[1024,64]{1,0:T(8,128)} %bitcast.16, bf16[1024,2048]{1,0:T(8,128)(2,1)} %bitcast.11, bf16[2048,256]{1,0:T(8,128)(2,1)} %bitcast.17, f32[1,256]{1,0:T(1,128)} %bias_ref.2), custom_call_target="tpu_custom_call" | custom-call | tf_op jit(solution)/shard_map/pallas_call | solution.py:35
  7.8 107.5 %shard_map.87 = (f32[16,2048]{1,0:T(8,128)}, bf16[8,128,2048]{2,1,0:T(8,128)(2,1)}, bf16[8,128,1024]{2,1,0:T(8,128)(2,1)}) custom-call(bf16[8,128,256]{2,1,0:T(8,128)(2,1)} %bitcast.15, bf16[1024,2048]{1,0:T(8,128)(2,1)} %bitcast.10, f32[1,2048]{1,0:T(1,128)} %bias_ref.3, bf16[16,2048]{1,0:T(8,128)(2,1)} %bitcast.19), custom_call_target="tpu_custom_call" | custom-call | tf_op jit(solution)/shard_map/pallas_call | solution.py:415
  115.3 0.0 copy-start
  115.3 10.7 %shard_map.88 = bf16[4,256,2048]{2,1,0:T(8,128)(2,1)} custom-call(bf16[1024,1024]{1,0:T(8,128)(2,1)} %bitcast.14, bf16[1024,2048]{1,0:T(8,128)(2,1)} %bitcast.13), custom_call_target="tpu_custom_call" | custom-call | tf_op jit(solution)/shard_map/pallas_call | solution.py:63
  126.0 0.0 copy-done
  126.0 0.7 copy.11
Async XLA Ops:
  115.3 10.7 %copy-start = (f32[16,2048]{1,0:T(8,128)S(1)}, f32[16,2048]{1,0:T(8,128)}, u32[]{:S(2)}) copy-start(f32[16,2048]{1,0:T(8,128)} %get-tuple-element.5) | copy-start | bytes 393220

commit v2 on v0

v2 whole, which is shorter than its diff:
```python
import jax
import jax.numpy as jnp
from jax import lax
from jax.experimental import pallas as pl
from jax.experimental.pallas import tpu as pltpu
from jax.sharding import PartitionSpec as P

MESH = pl.DeviceIdType.MESH
F32, BF16 = jnp.float32, jnp.bfloat16
NZ, NX, NY = 8, 4, 2
UP, DN = 0, 1


def grad_kernel(turned_ref, err_ref, out_ref):
    layers, width, cols = out_ref.shape
    product = jnp.dot(turned_ref[...], err_ref[...], preferred_element_type=F32)
    out_ref[...] = product.astype(BF16).reshape(layers, width, cols)


def grads_of(turned, err, layers):
    stacked, tokens = turned.shape
    model = err.shape[1]
    block = 256
    return pl.pallas_call(
        grad_kernel,
        grid=(model // block,),
        out_shape=jax.ShapeDtypeStruct((layers, stacked // layers, model), BF16),
        in_specs=[
            pl.BlockSpec((stacked, tokens), lambda i: (0, 0)),
            pl.BlockSpec((tokens, block), lambda i: (0, i)),
        ],
        out_specs=pl.BlockSpec((layers, stacked // layers, block), lambda i: (0, 0, i)),
    )(turned, err)


class Ring:
    def __init__(self, size, index, device, sends, recvs):
        self.size, self.index, self.device = size, index, device
        self.sends, self.recvs = sends, recvs
        self.far = size // 2
        self.started = []

    def at(self, offset):
        return lax.rem(self.index + offset + self.size, self.size)

    def copy(self, way, half, step, src, dst):
        toward = self.at(1 if way == UP else -1)
        return pltpu.make_async_remote_copy(
            src_ref=src,
            dst_ref=dst,
            send_sem=self.sends.at[way, half, step - 1],
            recv_sem=self.recvs.at[way, half, step - 1],
            device_id=self.device(toward),
            device_id_type=MESH,
        )

    def go(self, *what):
        copy = self.copy(*what)
        copy.start()
        self.started.append(copy)

    def drain(self):
        for copy in self.started:
            copy.wait_send()

    def reach(self, way, half):
        return self.far if way == half else self.far - 1


LONG, SHORT = ((UP, 0), (DN, 1)), ((UP, 1), (DN, 0))
STREAMS = ((UP, 0), (DN, 1), (UP, 1), (DN, 0))


class Reduce(Ring):
    def __init__(self, size, index, device, sends, recvs, own, held):
        super().__init__(size, index, device, sends, recvs)
        self.own, self.held = own, held

    def slot(self, way, half, step):
        return self.held.at[way, half, step - 1]

    def first(self, streams=STREAMS):
        for way, half in streams:
            far = self.reach(way, half)
            dest = self.at(far if way == UP else -far)
            self.go(way, half, far, self.own(dest, half), self.slot(way, half, far))

    def arrive(self, way, half, step):
        slot = self.slot(way, half, step)
        self.copy(way, half, step, slot, slot).wait_recv()
        return slot

    def pass_on(self, way, half, step):
        slot = self.arrive(way, half, step + 1)
        dest = self.at(step if way == UP else -step)
        own = self.own(dest, half)
        slot[...] = (slot[...].astype(F32) + own[...].astype(F32)).astype(BF16)
        self.go(way, half, step, slot, self.slot(way, half, step))

    def both(self, streams, step):
        for way, half in streams:
            self.pass_on(way, half, step)

    def total(self, half):
        up = self.arrive(UP, half, 1)
        down = self.arrive(DN, half, 1)
        own = self.own(self.index, half)
        return own[...].astype(F32) + (up[...].astype(F32) + down[...].astype(F32))


class Gather(Ring):
    def __init__(self, size, index, device, sends, recvs, view):
        super().__init__(size, index, device, sends, recvs)
        self.view = view

    def first(self, streams=STREAMS):
        for way, half in streams:
            block = self.view(self.index, half)
            self.go(way, half, 1, block, block)

    def arrive(self, way, half, step):
        block = self.view(self.at(-step if way == UP else step), half)
        self.copy(way, half, step, block, block).wait_recv()
        return block

    def pass_on(self, way, half, step):
        if step <= self.reach(way, half):
            block = self.arrive(way, half, step - 1)
            self.go(way, half, step, block, block)

    def spread(self, step):
        for way, half in STREAMS:
            self.pass_on(way, half, step)

    def last(self, streams=STREAMS):
        for way, half in streams:
            self.arrive(way, half, self.reach(way, half))


BLOCK = 128


def step_kernel(
    act_ref, resid_hbm, enc_hbm, enc_bias_ref, dec_hbm, dec_bias_ref, target_ref,
    err_ref, full_ref, turned_ref,
    resid, enc, dec, cat, part, mid_a, mid_b, end_a, end_b,
    held_az, held_ax, held_bx, held_bz, give_a, give_b, take_a, take_b,
    load, pair_send, pair_recv,
    s_az, r_az, s_ax, r_ax, s_bx, r_bx, s_bz, r_bz,
    g_ax, h_ax, g_az, h_az, g_bz, h_bz, g_bx, h_bx,
    y_send, y_recv,
):
    feat, pair = lax.axis_index("feat"), lax.axis_index("pair")
    z, x, y = feat // (NX * NY), lax.rem(feat // NY, NX), lax.rem(feat, NY)
    width = enc.shape[1]
    cut = mid_a.shape[1]
    cols_a, cols_b = pl.ds(0, cut), pl.ds(cut, part.shape[2] - cut)

    near_z = lambda by: lax.rem(z + by + NZ, NZ)
    near_x = lambda by: lax.rem(x + by + NX, NX)
    order = [near_z(by) for by in (4, 3, -3, 2, -2, 1, -1, 0)]

    enc_copy = pltpu.make_async_copy(enc_hbm, enc, load.at[NZ])
    dec_copy = pltpu.make_async_copy(dec_hbm, dec, load.at[NZ + 1])
    resid_copies = [
        pltpu.make_async_copy(
            resid_hbm.at[pl.ds(pl.multiple_of(o * BLOCK, BLOCK), BLOCK)], resid.at[k], load.at[k]
        )
        for k, o in enumerate(order)
    ]
    enc_copy.start()
    for copy in resid_copies[:2]:
        copy.start()
    dec_copy.start()
    for copy in resid_copies[2:]:
        copy.start()

    def spot(zz, xx, yy):
        return ((zz * NX + xx) * NY + yy, pair)

    along_z = lambda other: spot(other, x, y)
    along_x = lambda other: spot(z, other, y)
    across = spot(z, x, 1 - y)
    core_mate = (feat, pair + 1 - 2 * lax.rem(pair, 2))
    chip_mate = (feat, lax.rem(pair + 2, 4))

    barrier = pltpu.get_barrier_semaphore()
    greeted = (
        along_z(near_z(1)), along_z(near_z(-1)), along_x(near_x(1)), along_x(near_x(-1)),
        across, core_mate, chip_mate,
    )
    for device in greeted:
        pl.semaphore_signal(barrier, inc=1, device_id=device, device_id_type=MESH)

    for slot in range(1, 4):

        @pl.when(pair < slot)
        def _():
            cat[:, :, slot * width : (slot + 1) * width] = jnp.zeros((NZ, BLOCK, width), BF16)

    pl.semaphore_wait(barrier, len(greeted))

    low_chip, low_core = pair < 2, lax.rem(pair, 2) == 0
    relayed = lax.rem(pair, 2)

    def piece(slot, k):
        return cat.at[order[k], :, pl.ds(pl.multiple_of(slot * width, width), width)]

    def send_piece(kind, slot, k, device):
        return pltpu.make_async_remote_copy(
            src_ref=piece(slot, k), dst_ref=piece(slot, k),
            send_sem=pair_send.at[kind, k], recv_sem=pair_recv.at[slot, k],
            device_id=device, device_id_type=MESH,
        )

    def await_piece(slot, k):
        send_piece(0, slot, k, core_mate).wait_recv()

    def values(k):
        resid_copies[k].wait()
        if k == 0:
            enc_copy.wait()
        tokens = pl.ds(pl.multiple_of(order[k] * BLOCK, BLOCK), BLOCK)
        local = act_ref[:, tokens] - feat * width
        word = lax.shift_right_arithmetic(local, 5)
        bit = lax.shift_left(jnp.int32(1), local & 31)
        words = [
            jnp.sum(jnp.where(word == w, bit, 0), axis=0, keepdims=True)
            for w in range(width // 32)
        ]
        spread = jnp.concatenate([jnp.broadcast_to(w, (32, BLOCK)) for w in words], axis=0)
        place = lax.broadcasted_iota(jnp.int32, (width, BLOCK), 0) & 31
        chosen = (lax.shift_right_logical(spread, place) & 1).astype(F32).T
        pre = jnp.dot(resid[k], enc[...], preferred_element_type=F32) + enc_bias_ref[...]
        found = jnp.where(chosen > 0.5, jnp.maximum(pre, 0.0), 0.0).astype(BF16)
        piece(pair, k)[...] = found

        @pl.when(low_chip)
        def _():
            send_piece(0, pair, k, chip_mate).start()

        @pl.when(low_core)
        def _():
            send_piece(1, pair, k, core_mate).start()

    def relay(*ks):
        @pl.when(jnp.logical_not(low_chip))
        def _():
            for k in ks:
                await_piece(relayed, k)
                send_piece(2, relayed, k, core_mate).start()

    def decode(*ks):
        if ks[0] == 0:
            dec_copy.wait()

        @pl.when(jnp.logical_not(low_chip))
        def _():
            for k in ks:
                await_piece(1 - relayed, k)

        for holder, slot in ((1, 0), (3, 2)):

            @pl.when(pair == holder)
            def _():
                for k in ks:
                    await_piece(slot, k)

        step = 512

        @pl.loop(0, part.shape[2] // step)
        def _(i):
            cols = pl.ds(pl.multiple_of(i * step, step), step)
            rows = jnp.concatenate([cat[order[k]] for k in ks], axis=0)
            product = jnp.dot(rows, dec[:, cols], preferred_element_type=F32).astype(BF16)
            for n, k in enumerate(ks):
                part[order[k], :, cols] = product[n * BLOCK : (n + 1) * BLOCK]

    def rows16(index, half):
        return pl.ds(pl.multiple_of(index * 32 + half * 16, 16), 16)

    az = Reduce(NZ, z, along_z, s_az, r_az, lambda i, h: part.at[i, pl.ds(h * 64, 64), cols_a], held_az)
    ax = Reduce(NX, x, along_x, s_ax, r_ax, lambda i, h: mid_a.at[rows16(i, h)], held_ax)
    bx = [
        Reduce(
            NX, x, along_x, s_bx.at[k], r_bx.at[k],
            lambda i, h, o=o: part.at[o, rows16(i, h), cols_b], held_bx.at[k],
        )
        for k, o in enumerate(order)
    ]
    bz = Reduce(NZ, z, along_z, s_bz, r_bz, lambda i, h: mid_b.at[i, pl.ds(h * 16, 16)], held_bz)

    def settle(*ks):
        for k in ks:
            for half in range(2):
                mid_b[order[k], half * 16 : half * 16 + 16] = bx[k].total(half).astype(BF16)

    for k in range(3):
        values(k)
    relay(0)
    values(3)
    values(4)
    relay(1, 2)
    decode(0)
    az.first(LONG)
    bx[0].first()
    values(5)
    values(6)
    relay(3, 4)
    decode(1, 2)
    az.first(SHORT)
    bx[1].first()
    bx[2].first()
    values(7)
    relay(5, 6)
    az.both(LONG, 3)
    decode(3, 4)
    bx[3].first()
    bx[4].first()
    bx[0].both(LONG, 1)
    relay(7)
    az.both(SHORT, 2)
    decode(5, 6)
    bx[5].first()
    bx[6].first()
    bx[1].both(LONG, 1)
    bx[2].both(LONG, 1)
    az.both(LONG, 2)
    decode(7)
    bx[7].first()
    settle(0)
    bz.first(LONG)
    bx[3].both(LONG, 1)
    bx[4].both(LONG, 1)
    az.both(SHORT, 1)
    settle(1, 2)
    bz.first(SHORT)
    bz.both(LONG, 3)
    bx[5].both(LONG, 1)
    bx[6].both(LONG, 1)
    az.both(LONG, 1)
    bx[7].both(LONG, 1)
    settle(3, 4)
    bz.both(SHORT, 2)
    bz.both(LONG, 2)
    settle(5, 6)
    bz.both(SHORT, 1)
    for half in range(2):
        mid_a[half * 64 : half * 64 + 64] = az.total(half).astype(BF16)
    ax.first()
    bz.both(LONG, 1)
    settle(7)
    ax.both(LONG, 1)

    def over_y(which, src, dst):
        return pltpu.make_async_remote_copy(
            src_ref=src, dst_ref=dst, send_sem=y_send.at[which], recv_sem=y_recv.at[which],
            device_id=across, device_id_type=MESH,
        )

    last_copies = []
    for which, ring, end, give, take in ((0, ax, end_a, give_a, take_a), (1, bz, end_b, give_b, take_b)):
        for half in range(2):
            end[half] = ring.total(half)
            give[half] = end[half].astype(BF16)
        copy = over_y(which, give.at[1 - y], take)
        copy.start()
        last_copies.append(copy)

    def rows_of(xx, half):
        return rows16(xx, y if half == 0 else 1 - y)

    gax = Gather(NX, x, along_x, g_ax, h_ax, lambda i, h: full_ref.at[z, rows_of(i, h), cols_a])
    gbz = Gather(NZ, z, along_z, g_bz, h_bz, lambda i, h: full_ref.at[i, rows_of(x, h), cols_b])
    gaz = {
        by: Gather(
            NZ, z, along_z, g_az.at[n], h_az.at[n],
            lambda i, h, xx=near_x(by): full_ref.at[i, rows_of(xx, h), cols_a],
        )
        for n, by in enumerate((0, -1, 1, 2))
    }
    gbx = {
        by: Gather(
            NX, x, along_x, g_bx.at[n], h_bx.at[n],
            lambda i, h, zz=near_z(by): full_ref.at[zz, rows_of(i, h), cols_b],
        )
        for n, by in enumerate((0, -1, 1, -2, 2, -3, 3, 4))
    }
    mine, theirs = ((UP, 0), (DN, 0)), ((UP, 1), (DN, 1))
    y_copies = []
    for which, end, take, first, then in ((0, end_a, take_a, gax, gaz), (1, end_b, take_b, gbz, gbx)):
        last_copies[which].wait_recv()
        cols = slice(0, cut) if which == 0 else slice(cut, part.shape[2])
        error = end[y] + take[...].astype(F32) + dec_bias_ref[:, cols] - target_ref[:, cols].astype(F32)
        full_ref[z, rows_of(x, 0), cols] = error.astype(BF16)
        block = full_ref.at[z, rows_of(x, 0), cols]
        copy = over_y(2 + which, block, block)
        copy.start()
        y_copies.append(copy)
        first.first(mine)
        then[0].first(mine)
        err_ref[:, cols] = error
    for which, first, then in ((0, gax, gaz), (1, gbz, gbx)):
        cols = cols_a if which == 0 else cols_b
        block = full_ref.at[z, rows_of(x, 1), cols]
        over_y(2 + which, block, block).wait_recv()
        first.first(theirs)
        then[0].first(theirs)

    gax.pass_on(UP, 0, 2)
    gax.last(((UP, 1),))
    gaz[-1].first()
    gax.pass_on(DN, 1, 2)
    gax.last(((DN, 0),))
    gaz[1].first()
    gbz.spread(2)
    gbx[-1].first()
    gbx[1].first()
    gaz[0].spread(2)
    gax.last(LONG)
    gaz[2].first()
    gbx[0].spread(2)
    gbz.spread(3)
    gbx[-2].first()
    gbx[2].first()
    for n in range(4):
        tokens = pl.ds(n * 256, 256)
        turned_ref[:, tokens] = cat[2 * n : 2 * n + 2].reshape(256, -1).T
        if n == 0:
            gaz[-1].spread(2)
            gaz[1].spread(2)
            gbx[-1].spread(2)
            gbx[1].spread(2)
        if n == 1:
            gbz.spread(4)
            gbz.last(SHORT)
            gbx[-3].first()
            gbx[3].first()
            gaz[0].spread(3)
        if n == 2:
            gaz[2].spread(2)
            gbz.last(LONG)
            gbx[4].first()
            gaz[-1].spread(3)
            gaz[1].spread(3)
    gbx[-2].spread(2)
    gbx[2].spread(2)
    gaz[0].spread(4)
    gaz[2].spread(3)
    gbx[-3].spread(2)
    gbx[3].spread(2)
    gaz[-1].spread(4)
    gaz[1].spread(4)
    gbx[4].spread(2)
    gaz[2].spread(4)
    for by in (0, -1, 1, -2, 2, -3, 3, 4):
        gbx[by].last()
    for by in (0, -1, 1, 2):
        gaz[by].last()

    for ring in (az, ax, bz, *bx, gax, gbz, *gaz.values(), *gbx.values()):
        ring.drain()
    for copy in last_copies + y_copies:
        copy.wait_send()

    @pl.when(low_chip)
    def _():
        for k in range(NZ):
            send_piece(0, pair, k, chip_mate).wait_send()

    @pl.when(low_core)
    def _():
        for k in range(NZ):
            send_piece(1, pair, k, core_mate).wait_send()

    @pl.when(jnp.logical_not(low_chip))
    def _():
        for k in range(NZ):
            send_piece(2, relayed, k, core_mate).wait_send()


def step(active, resid, enc, enc_bias, dec, dec_bias, target):
    tokens, model = resid.shape
    width, stacked = enc.shape[1], dec.shape[0]
    cut = 896
    rest = model - cut
    dma, vmem = pltpu.SemaphoreType.DMA, pltpu.VMEM
    here, there = pl.BlockSpec(memory_space=pltpu.VMEM), pl.BlockSpec(memory_space=pl.ANY)
    long, short = (2, 2, NZ // 2), (2, 2, NX // 2)
    return pl.pallas_call(
        step_kernel,
        out_shape=(
            jax.ShapeDtypeStruct(target.shape, F32),
            jax.ShapeDtypeStruct((NZ, BLOCK, model), BF16),
            jax.ShapeDtypeStruct((stacked, tokens), BF16),
        ),
        in_specs=[here, there, there, here, there, here, here],
        out_specs=(here,) * 3,
        scratch_shapes=[
            vmem((NZ, BLOCK, model), BF16),
            vmem((model, width), BF16),
            vmem((stacked, model), BF16),
            vmem((NZ, BLOCK, stacked), BF16),
            vmem((NZ, BLOCK, model), BF16),
            vmem((BLOCK, cut), BF16),
            vmem((NZ, 32, rest), BF16),
            vmem((2, 16, cut), F32),
            vmem((2, 16, rest), F32),
            vmem((*long, 64, cut), BF16),
            vmem((*short, 16, cut), BF16),
            vmem((NZ, *short, 16, rest), BF16),
            vmem((*long, 16, rest), BF16),
            vmem((2, 16, cut), BF16),
            vmem((2, 16, rest), BF16),
            vmem((16, cut), BF16),
            vmem((16, rest), BF16),
            dma((NZ + 2,)),
            dma((3, NZ)),
            dma((4, NZ)),
            dma(long), dma(long), dma(short), dma(short),
            dma((NZ, *short)), dma((NZ, *short)), dma(long), dma(long),
            dma(short), dma(short), dma((4, *long)), dma((4, *long)),
            dma(long), dma(long), dma((NZ, *short)), dma((NZ, *short)),
            dma((4,)),
            dma((4,)),
        ],
        compiler_params=pltpu.CompilerParams(
            collective_id=0, has_side_effects=True, vmem_limit_bytes=60 * 1024 * 1024
        ),
    )(active, resid, enc, enc_bias, dec, dec_bias, target)


def local(resid, enc_weight, enc_bias, active, dec_weight, dec_bias, target):
    layers, width, model = dec_weight.shape[1:]
    tokens = resid.shape[1]
    error, full, turned = step(
        active[0].T, resid[0], enc_weight[0], enc_bias,
        dec_weight[0].reshape(layers * width, model), dec_bias, target[0],
    )
    grads = grads_of(turned, full.reshape(tokens, model), layers)
    return error[None], grads[None]


def solution(mesh):
    in_specs = (
        P("pair", None, None),
        P("pair", None, "feat"),
        P("pair", "feat"),
        P("pair", None, None),
        P("pair", None, "feat", None),
        P("pair", None),
        P("pair", "feat", None),
    )
    out_specs = (P("pair", "feat", None), P("pair", None, "feat", None))
    return jax.shard_map(local, mesh=mesh, in_specs=in_specs, out_specs=out_specs, check_vma=False)
```

time: 628 us -> 102 us (0.16)
  waiting for transfers between devices: 550 us -> 0 us
  Pallas kernels: 0 us -> 100 us
  matrix products: 42.1 us -> 0 us
  between operations: 13.8 us -> 0.65 us
  other arithmetic: 13.1 us -> 0 us
  local copies, waits for them, and re-layouts: 8.05 us -> 0.66 us
    reduce_scatter x1 -> x0, waiting for transfers between devices: 394 us -> none  [local(): lax.psum_scatter(lax.fori_loop(0, pair_index + 1, add_source, jnp.zeros((...]
    all_gather x2 -> x0, waiting for transfers between devices: 156 us -> none  [the longest x1 123 us: local(): lax.all_gather(error_shard.astype(jnp.bfloat16), 'feat', axis=0, tiled=True)]
    pallas_call x0 -> x2, Pallas kernels: none -> 100 us  [the longest x1 90.1 us: step(): pl.pallas_call(step_kernel, out_shape=(jax.ShapeDtypeStruct(target.shape,...]
    dot_general x7 -> x0, matrix products: 42.1 us -> none  [the longest x3 24.6 us: add_source(): jnp.dot(left_rows, weight_rows, preferred_element_type=jnp.float32)]
    reduce_or x1 -> x0, other arithmetic: 11.5 us -> none  [local(): chosen = jnp.any(active[0][:, :, None] == columns[None, None, :], axis=1)]
    broadcast_in_dim x2 -> x0, local copies, waits for them, and re-layouts: 6.81 us -> none  [the longest x1 4.28 us: local(): jnp.zeros((shard_rows * lax.axis_size('feat'), model_width), jnp.float32)]
  transfers between devices with their start and end apart: 3 -> 0, of which waited for: 3 -> 0; matrix products, arithmetic and copies ran while one was open for 0% -> 0% of each run, Pallas kernels for 0% -> 0%
where the time goes in v2:
time: 102 us; the launch traced here: 101 us
  Pallas kernels  100 us (98%)
    pallas_call x1, Pallas kernels, step(): pl.pallas_call(step_kernel, out_shape=(jax.ShapeDtypeStruct(target.shape,...  90.1 us
    pallas_call x1, Pallas kernels, grads_of(): pl.pallas_call(grad_kernel, grid=(model // block,), out_shape=jax.ShapeDt...  10 us

profile of v2, /device:TPU:8, one launch (start us, length us, event | category | flops | bytes accessed | tf_op | source)
XLA Modules:
  0.0 101.5 jit_solution(10704981305227163957)
XLA Ops:
  0.6 90.1 %shard_map.86 = (f32[16,2048]{1,0:T(8,128)}, bf16[8,128,2048]{2,1,0:T(8,128)(2,1)}, bf16[1024,1024]{1,0:T(8,128)(2,1)}) custom-call(s32[64,1024]{1,0:T(8,128)} %bitcast.15, bf16[1024,2048]{1,0:T(8,128)(2,1)} %bitcast.10, bf16[2048,256]{1,0:T(8,128)(2,1)} %bitcast.14, f32[1,256]{1,0:T(1,128)} %enc_bias_ref.1, bf16[1024,2048]{1,0:T(8,128)(2,1)} %bitcast.11, ...), custom_call_target="tpu_custom_call" | custom-call | tf_op jit(solution)/shard_map/pallas_call | solution.py:490
  90.8 0.0 copy-start
  90.8 10.0 %shard_map.87 = bf16[4,256,2048]{2,1,0:T(8,128)(2,1)} custom-call(bf16[1024,1024]{1,0:T(8,128)(2,1)} %get-tuple-element.6.turned_ref, bf16[1024,2048]{1,0:T(8,128)(2,1)} %bitcast.13), custom_call_target="tpu_custom_call" | custom-call | tf_op jit(solution)/shard_map/pallas_call | solution.py:24
  100.8 0.0 copy-done
  100.8 0.7 copy.10
Async XLA Ops:
  90.8 10.0 %copy-start = (f32[16,2048]{1,0:T(8,128)S(1)}, f32[16,2048]{1,0:T(8,128)}, u32[]{:S(2)}) copy-start(f32[16,2048]{1,0:T(8,128)} %get-tuple-element.5) | copy-start | bytes 393220

commit v3 on v0

v3 whole, which is shorter than its diff:
```python
import jax
import jax.numpy as jnp
from jax import lax
from jax.experimental import pallas as pl
from jax.experimental.pallas import tpu as pltpu
from jax.sharding import PartitionSpec as P

MESH = pl.DeviceIdType.MESH
F32, BF16 = jnp.float32, jnp.bfloat16
NZ, NX, NY = 8, 4, 2
UP, DN = 0, 1


BLOCK = 128
SETS = ((384, 640), (512, 512))
GROUPS = ((0,), (1, 2), (3, 4), (5, 6), (7,))
DISTANCES = (4, 3, -3, 2, -2, 1, -1, 0)
LONG, SHORT = ((UP, 0), (DN, 1)), ((UP, 1), (DN, 0))
STREAMS = LONG + SHORT
WIRE, LATENCY = 47e3, 1.9


class Plan:
    def __init__(self):
        self.steps, self.sender = [], {}

    def add(self, run, took, after=(), needs=(), sends=(), bias=0.0):
        me = len(self.steps)
        self.steps.append((run, took, tuple(after), tuple(needs), tuple(sends), bias))
        for key, _, _ in sends:
            self.sender[key] = me
        return me

    def order(self):
        count = len(self.steps)
        follows = [[] for _ in range(count)]
        ahead = [0] * count
        size = {key: n for step in self.steps for key, _, n in step[4]}
        for me, (_, _, after, needs, _, _) in enumerate(self.steps):
            for other in after:
                follows[other].append((me, 0.0))
            for key in needs:
                follows[self.sender[key]].append((me, LATENCY + size[key] / WIRE))
            ahead[me] = len(after) + len(needs)
        level, left = [0.0] * count, ahead[:]
        queue = [me for me in range(count) if left[me] == 0]
        for me in queue:
            for other, _ in follows[me]:
                left[other] -= 1
                if left[other] == 0:
                    queue.append(other)
        for me in reversed(queue):
            level[me] = self.steps[me][1] + max((d + level[o] for o, d in follows[me]), default=0.0)
        now, free, landed, done, result = 0.0, {}, {}, [False] * count, []
        waiting = list(range(count))
        while waiting:
            best = None
            for me in waiting:
                _, _, after, needs, _, bias = self.steps[me]
                if all(done[o] for o in after) and all(key in landed for key in needs):
                    at = max([now] + [landed[key] for key in needs])
                    rank = (at > now, at if at > now else 0.0, -level[me] - bias, me)
                    if best is None or rank < best[0]:
                        best = (rank, me, at)
            _, me, at = best
            now = at + self.steps[me][1]
            for key, link, n in self.steps[me][4]:
                start = max(now, free.get(link, 0.0))
                free[link] = start + n / WIRE
                landed[key] = free[link] + LATENCY
            done[me] = True
            waiting.remove(me)
            result.append(me)
        self.length = now
        return result

    def run(self):
        for me in self.order():
            self.steps[me][0]()


class Ring:
    def __init__(self, name, size, index, device, link, nbytes, sends, recvs):
        self.name, self.size, self.index, self.device = name, size, index, device
        self.link, self.nbytes, self.sends, self.recvs = link, nbytes, sends, recvs
        self.far = size // 2
        self.started = []

    def at(self, offset):
        return lax.rem(self.index + offset + self.size, self.size)

    def copy(self, way, half, step, src, dst):
        toward = self.at(1 if way == UP else -1)
        return pltpu.make_async_remote_copy(
            src_ref=src,
            dst_ref=dst,
            send_sem=self.sends.at[way, half, step - 1],
            recv_sem=self.recvs.at[way, half, step - 1],
            device_id=self.device(toward),
            device_id_type=MESH,
        )

    def go(self, *what):
        copy = self.copy(*what)
        copy.start()
        self.started.append(copy)

    def drain(self):
        for copy in self.started:
            copy.wait_send()

    def reach(self, way, half):
        return self.far if way == half else self.far - 1

    def key(self, way, half, step):
        return (*self.name, way, half, step)

    def message(self, way, half, step):
        return (self.key(way, half, step), self.link + str(way), self.nbytes)


class Reduce(Ring):
    def __init__(self, *ring, own, held):
        super().__init__(*ring)
        self.own, self.held = own, held

    def slot(self, way, half, step):
        return self.held.at[way, half, step - 1]

    def first(self, way, half):
        far = self.reach(way, half)
        dest = self.at(far if way == UP else -far)
        self.go(way, half, far, self.own(dest, half), self.slot(way, half, far))

    def arrive(self, way, half, step):
        slot = self.slot(way, half, step)
        self.copy(way, half, step, slot, slot).wait_recv()
        return slot

    def pass_on(self, way, half, step):
        slot = self.arrive(way, half, step + 1)
        own = self.own(self.at(step if way == UP else -step), half)
        slot[...] = (slot[...].astype(F32) + own[...].astype(F32)).astype(BF16)
        self.go(way, half, step, slot, self.slot(way, half, step))

    def total(self, half):
        up = self.arrive(UP, half, 1)
        down = self.arrive(DN, half, 1)
        own = self.own(self.index, half)
        return own[...].astype(F32) + (up[...].astype(F32) + down[...].astype(F32))

    def plan(self, plan, ready, finish, took, bias):
        for way, half in STREAMS:
            sign = 1 if way == UP else -1
            far = self.reach(way, half)
            plan.add(
                lambda w=way, h=half: self.first(w, h), 0.04,
                after=ready(sign * far, half), sends=[self.message(way, half, far)], bias=bias,
            )
            for step in range(far - 1, 0, -1):
                plan.add(
                    lambda w=way, h=half, s=step: self.pass_on(w, h, s), took,
                    after=ready(sign * step, half), needs=[self.key(way, half, step + 1)],
                    sends=[self.message(way, half, step)], bias=bias,
                )
        return [
            plan.add(
                lambda h=half: finish(h, self.total(h)), 1.5 * took,
                after=ready(0, half), needs=[self.key(way, half, 1) for way in (UP, DN)], bias=bias,
            )
            for half in range(2)
        ]


class Gather(Ring):
    def __init__(self, *ring, view):
        super().__init__(*ring)
        self.view = view

    def first(self, half):
        for way in (UP, DN):
            block = self.view(self.index, half)
            self.go(way, half, 1, block, block)

    def first_messages(self, half):
        return [self.message(way, half, 1) for way in (UP, DN)]

    def arrive(self, way, half, step):
        block = self.view(self.at(-step if way == UP else step), half)
        self.copy(way, half, step, block, block).wait_recv()
        if step < self.reach(way, half):
            self.go(way, half, step + 1, block, block)

    def plan(self, plan, then=None):
        added = []
        for way, half in STREAMS:
            for step in range(1, self.reach(way, half) + 1):
                sends = [self.message(way, half, step + 1)] if step < self.reach(way, half) else []
                ring = then(-step if way == UP else step) if then else None
                if ring:
                    sends += ring.first_messages(half)

                def run(w=way, h=half, s=step, ring=ring):
                    self.arrive(w, h, s)
                    if ring:
                        ring.first(h)

                added.append(plan.add(run, 0.06 + 0.03 * len(sends), needs=[self.key(way, half, step)], sends=sends))
        return added


def step_kernel(
    act_ref, resid_hbm, enc_hbm, enc_bias_ref, dec_hbm, dec_bias_ref, target_ref,
    err_ref, grads_hbm,
    resid, enc, dec, cat, part, full, turned, grads,
    mid_a, mid_b, end, give, take, held_az, held_ax, held_bx, held_bz,
    load, store, pair_send, pair_recv,
    s_az, r_az, s_ax, r_ax, s_bx, r_bx, s_bz, r_bz,
    g_ax, h_ax, g_az, h_az, g_bz, h_bz, g_bx, h_bx,
    y_send, y_recv,
):
    feat, pair = lax.axis_index("feat"), lax.axis_index("pair")
    z, x, y = feat // (NX * NY), lax.rem(feat // NY, NX), lax.rem(feat, NY)
    width = enc.shape[1]

    near_z = lambda by: lax.rem(z + by + NZ, NZ)
    near_x = lambda by: lax.rem(x + by + NX, NX)
    order = [near_z(by) for by in DISTANCES]
    place_of = {by: k for k, by in enumerate(DISTANCES)}

    enc_copy = pltpu.make_async_copy(enc_hbm, enc, load.at[NZ])
    dec_copy = pltpu.make_async_copy(dec_hbm, dec, load.at[NZ + 1])
    resid_copies = [
        pltpu.make_async_copy(
            resid_hbm.at[pl.ds(pl.multiple_of(o * BLOCK, BLOCK), BLOCK)], resid.at[k], load.at[k]
        )
        for k, o in enumerate(order)
    ]
    enc_copy.start()
    for copy in resid_copies[:3]:
        copy.start()
    dec_copy.start()
    for copy in resid_copies[3:]:
        copy.start()

    def spot(zz, xx, yy):
        return ((zz * NX + xx) * NY + yy, pair)

    along_z = lambda other: spot(other, x, y)
    along_x = lambda other: spot(z, other, y)
    across = spot(z, x, 1 - y)
    core_mate = (feat, pair + 1 - 2 * lax.rem(pair, 2))
    chip_mate = (feat, lax.rem(pair + 2, 4))

    barrier = pltpu.get_barrier_semaphore()
    greeted = (
        along_z(near_z(1)), along_z(near_z(-1)), along_x(near_x(1)), along_x(near_x(-1)),
        across, core_mate, chip_mate,
    )
    for device in greeted:
        pl.semaphore_signal(barrier, inc=1, device_id=device, device_id_type=MESH)

    for slot in range(1, 4):

        @pl.when(pair < slot)
        def _():
            cat[:, :, slot * width : (slot + 1) * width] = jnp.zeros((NZ, BLOCK, width), BF16)

    pl.semaphore_wait(barrier, len(greeted))
    plan = Plan()

    low_chip, low_core = pair < 2, lax.rem(pair, 2) == 0
    relayed = lax.rem(pair, 2)

    def piece(slot, k):
        return cat.at[order[k], :, pl.ds(pl.multiple_of(slot * width, width), width)]

    def send_piece(kind, slot, k, device):
        return pltpu.make_async_remote_copy(
            src_ref=piece(slot, k), dst_ref=piece(slot, k),
            send_sem=pair_send.at[kind, k], recv_sem=pair_recv.at[slot, k],
            device_id=device, device_id_type=MESH,
        )

    def await_piece(slot, k):
        send_piece(0, slot, k, core_mate).wait_recv()

    def chosen_of(k):
        tokens = pl.ds(pl.multiple_of(order[k] * BLOCK, BLOCK), BLOCK)
        local = act_ref[:, tokens] - feat * width
        word = lax.shift_right_arithmetic(local, 5)
        bit = lax.shift_left(jnp.int32(1), local & 31)
        words = [
            jnp.sum(jnp.where(word == w, bit, 0), axis=0, keepdims=True)
            for w in range(width // 32)
        ]
        spread = jnp.concatenate([jnp.broadcast_to(w, (32, BLOCK)) for w in words], axis=0)
        place = lax.broadcasted_iota(jnp.int32, (width, BLOCK), 0) & 31
        return (lax.shift_right_logical(spread, place) & 1).astype(F32).T

    def values(ks):
        for k in ks:
            resid_copies[k].wait()
        if ks[0] == 0:
            enc_copy.wait()
        rows = jnp.concatenate([resid[k] for k in ks], axis=0)
        pre = jnp.dot(rows, enc[...], preferred_element_type=F32) + enc_bias_ref[...]
        for n, k in enumerate(ks):
            kept = jnp.maximum(pre[n * BLOCK : (n + 1) * BLOCK], 0.0)
            piece(pair, k)[...] = jnp.where(chosen_of(k) > 0.5, kept, 0.0).astype(BF16)

        @pl.when(low_chip)
        def _():
            for k in ks:
                send_piece(0, pair, k, chip_mate).start()

        @pl.when(low_core)
        def _():
            for k in ks:
                send_piece(1, pair, k, core_mate).start()

    def relay(ks):
        @pl.when(jnp.logical_not(low_chip))
        def _():
            for k in ks:
                await_piece(relayed, k)
                send_piece(2, relayed, k, core_mate).start()

    def collect(ks):
        @pl.when(jnp.logical_not(low_chip))
        def _():
            for k in ks:
                await_piece(1 - relayed, k)

        for holder, slot in ((1, 0), (3, 2)):

            @pl.when(pair == holder)
            def _():
                for k in ks:
                    await_piece(slot, k)

    def decode(ks, c):
        if c == 0:
            if ks[0] == 0:
                dec_copy.wait()
            collect(ks)
        step = 512

        @pl.loop(2 * c, 2 * c + 2)
        def _(i):
            cols = pl.ds(pl.multiple_of(i * step, step), step)
            rows = jnp.concatenate([cat[order[k]] for k in ks], axis=0)
            product = jnp.dot(rows, dec[:, cols], preferred_element_type=F32).astype(BF16)
            for n, k in enumerate(ks):
                part[order[k], :, cols] = product[n * BLOCK : (n + 1) * BLOCK]

    decoded = [{}, {}]
    before = ()
    for ks in GROUPS:
        name = ("v", ks)
        before = [
            plan.add(
                lambda ks=ks: values(ks), 0.35 + 0.45 * len(ks),
                after=before, sends=[(name, "mate", 65536 * len(ks))], bias=100.0,
            )
        ]
        plan.add(lambda ks=ks: relay(ks), 0.1, needs=[name], sends=[(("r", ks), "core", 3000)], bias=200.0)
        last = ()
        for c in range(2):
            last = [
                plan.add(
                    lambda ks=ks, c=c: decode(ks, c), 0.35 + 0.3 * len(ks),
                    after=last, needs=[("r", ks)] if c == 0 else [], bias=40.0 - 40.0 * c,
                )
            ]
            for k in ks:
                decoded[c][k] = last[0]

    def turn(k):
        turned[:, pl.ds(pl.multiple_of(order[k] * BLOCK, BLOCK), BLOCK)] = cat[order[k]].T

    turns = [plan.add(lambda k=k: turn(k), 0.35, after=[decoded[1][k]]) for k in range(NZ)]

    def rows16(index, half):
        return pl.ds(pl.multiple_of(index * 32 + half * 16, 16), 16)

    def rows_of(xx, half):
        return rows16(xx, y if half == 0 else 1 - y)

    def over_y(which, src, dst):
        return pltpu.make_async_remote_copy(
            src_ref=src, dst_ref=dst, send_sem=y_send.at[which], recv_sem=y_recv.at[which],
            device_id=across, device_id_type=MESH,
        )

    rings, y_copies, arrived = [], [], {}
    base = 0
    for c, (wide_a, wide_b) in enumerate(SETS):
        bias = 40.0 - 40.0 * c
        at_a, at_b = slice(base, base + wide_a), slice(base + wide_a, base + wide_a + wide_b)
        cols_a, cols_b = pl.ds(base, wide_a), pl.ds(base + wide_a, wide_b)
        base += wide_a + wide_b

        az = Reduce(
            ("az", c), NZ, z, along_z, "z", 128 * wide_a, s_az.at[c], r_az.at[c],
            own=lambda i, h, cols=cols_a: part.at[i, pl.ds(h * 64, 64), cols], held=held_az[c],
        )
        ax = Reduce(
            ("ax", c), NX, x, along_x, "x", 32 * wide_a, s_ax.at[c], r_ax.at[c],
            own=lambda i, h, mid=mid_a[c]: mid.at[rows16(i, h)], held=held_ax[c],
        )
        bx = [
            Reduce(
                ("bx", c, k), NX, x, along_x, "x", 32 * wide_b, s_bx.at[c, k], r_bx.at[c, k],
                own=lambda i, h, o=o, cols=cols_b: part.at[o, rows16(i, h), cols], held=held_bx[c].at[k],
            )
            for k, o in enumerate(order)
        ]
        bz = Reduce(
            ("bz", c), NZ, z, along_z, "z", 32 * wide_b, s_bz.at[c], r_bz.at[c],
            own=lambda i, h, mid=mid_b[c]: mid.at[i, pl.ds(h * 16, 16)], held=held_bz[c],
        )
        rings += [az, ax, bz, *bx]

        def keep_a(half, value, mid=mid_a[c]):
            mid[half * 64 : half * 64 + 64] = value.astype(BF16)

        def keep_end(which):
            def keep(half, value):
                end[which][half] = value
                give[which][half] = value.astype(BF16)

            return keep

        def block_ready(by, half, c=c):
            return [decoded[c][0 if by == -4 else place_of[by]]]

        summed_a = az.plan(plan, block_ready, keep_a, 0.12, bias)
        ended_a = ax.plan(plan, lambda by, half: summed_a, keep_end(2 * c), 0.06, bias)
        summed_b = []
        for k in range(NZ):

            def keep_b(half, value, o=order[k], mid=mid_b[c]):
                mid[o, half * 16 : half * 16 + 16] = value.astype(BF16)

            summed_b.append(bx[k].plan(plan, lambda by, half, k=k: [decoded[c][k]], keep_b, 0.07, bias))
        ended_b = bz.plan(
            plan, lambda by, half: [summed_b[0 if by == -4 else place_of[by]][half]], keep_end(2 * c + 1), 0.07, bias
        )

        gax = Gather(
            ("gax", c), NX, x, along_x, "x", 32 * wide_a, g_ax.at[c], h_ax.at[c],
            view=lambda i, h, cols=cols_a: full.at[z, rows_of(i, h), cols],
        )
        gbz = Gather(
            ("gbz", c), NZ, z, along_z, "z", 32 * wide_b, g_bz.at[c], h_bz.at[c],
            view=lambda i, h, cols=cols_b: full.at[i, rows_of(x, h), cols],
        )
        gaz = {
            by: Gather(
                ("gaz", c, by), NZ, z, along_z, "z", 32 * wide_a, g_az.at[c, n], h_az.at[c, n],
                view=lambda i, h, xx=near_x(by), cols=cols_a: full.at[i, rows_of(xx, h), cols],
            )
            for n, by in enumerate((0, -1, 1, 2))
        }
        gbx = {
            by: Gather(
                ("gbx", c, by), NX, x, along_x, "x", 32 * wide_b, g_bx.at[c, n], h_bx.at[c, n],
                view=lambda i, h, zz=near_z(by), cols=cols_b: full.at[zz, rows_of(i, h), cols],
            )
            for n, by in enumerate((0, -1, 1, -2, 2, -3, 3, 4))
        }
        rings += [gax, gbz, *gaz.values(), *gbx.values()]

        for part_index, ended, cols, at, wide, first, then in (
            (0, ended_a, cols_a, at_a, wide_a, gax, gaz),
            (1, ended_b, cols_b, at_b, wide_b, gbz, gbx),
        ):
            which = 2 * c + part_index

            def cross(which=which):
                copy = over_y(which, give[which].at[1 - y], take[which])
                copy.start()
                y_copies.append(copy)

            crossed = plan.add(cross, 0.04, after=ended, sends=[(("y", which), "y", 32 * wide)], bias=bias)

            def settle(which=which, cols=cols, at=at, first=first, ring=then[0]):
                over_y(which, take[which], take[which]).wait_recv()
                rebuilt = end[which][y] + take[which][...].astype(F32)
                error = rebuilt + dec_bias_ref[:, at] - target_ref[:, at].astype(F32)
                block = full.at[z, rows_of(x, 0), cols]
                block[...] = error.astype(BF16)
                err_ref[:, at] = error
                copy = over_y(4 + which, block, block)
                copy.start()
                y_copies.append(copy)
                first.first(0)
                ring.first(0)

            settled = plan.add(
                settle, 0.25, after=[crossed], needs=[("y", which)],
                sends=[(("e", which), "y", 32 * wide), *first.first_messages(0), *then[0].first_messages(0)],
            )

            def greet(which=which, cols=cols, first=first, ring=then[0]):
                block = full.at[z, rows_of(x, 1), cols]
                over_y(4 + which, block, block).wait_recv()
                first.first(1)
                ring.first(1)

            greeted_y = plan.add(
                greet, 0.15, after=[settled], needs=[("e", which)],
                sends=[*first.first_messages(1), *then[0].first_messages(1)],
            )
            ends = [settled, greeted_y]
            if part_index == 0:
                ends += first.plan(plan, lambda by, then=then: then[2 if abs(by) == 2 else by])
            else:
                ends += first.plan(plan, lambda by, then=then: then[4 if abs(by) == 4 else by])
            for ring in then.values():
                ends += ring.plan(plan)
            arrived[which] = (at, ends)

    step = 256
    grad_copies = []
    for n in range(part.shape[2] // step):

        def grad(n=n):
            cols = slice(n * step, (n + 1) * step)
            rows = full[:, :, cols].reshape(-1, step)
            grads[:, cols] = jnp.dot(turned[...], rows, preferred_element_type=F32).astype(BF16)
            copy = pltpu.make_async_copy(
                grads.at[:, pl.ds(n * step, step)], grads_hbm.at[:, pl.ds(n * step, step)], store.at[n]
            )
            copy.start()
            grad_copies.append(copy)

        after = [*turns]
        for at, ends in arrived.values():
            if at.start < (n + 1) * step and at.stop > n * step:
                after += ends
        plan.add(grad, 0.75, after=after)

    plan.run()

    for ring in rings:
        ring.drain()
    for copy in y_copies:
        copy.wait_send()

    @pl.when(low_chip)
    def _():
        for k in range(NZ):
            send_piece(0, pair, k, chip_mate).wait_send()

    @pl.when(low_core)
    def _():
        for k in range(NZ):
            send_piece(1, pair, k, core_mate).wait_send()

    @pl.when(jnp.logical_not(low_chip))
    def _():
        for k in range(NZ):
            send_piece(2, relayed, k, core_mate).wait_send()

    for copy in grad_copies:
        copy.wait()


def step(active, resid, enc, enc_bias, dec, dec_bias, target):
    tokens, model = resid.shape
    width, stacked = enc.shape[1], dec.shape[0]
    dma, vmem = pltpu.SemaphoreType.DMA, pltpu.VMEM
    here, there = pl.BlockSpec(memory_space=pltpu.VMEM), pl.BlockSpec(memory_space=pl.ANY)
    long, short = (2, 2, NZ // 2), (2, 2, NX // 2)
    parts = [wide for pair in SETS for wide in pair]
    per_set = lambda shape: [dma((len(SETS), *shape))] * 2
    return pl.pallas_call(
        step_kernel,
        out_shape=(
            jax.ShapeDtypeStruct(target.shape, F32),
            jax.ShapeDtypeStruct((stacked, model), BF16),
        ),
        in_specs=[here, there, there, here, there, here, here],
        out_specs=(here, there),
        scratch_shapes=[
            vmem((NZ, BLOCK, model), BF16),
            vmem((model, width), BF16),
            vmem((stacked, model), BF16),
            vmem((NZ, BLOCK, stacked), BF16),
            vmem((NZ, BLOCK, model), BF16),
            vmem((NZ, BLOCK, model), BF16),
            vmem((stacked, tokens), BF16),
            vmem((stacked, model), BF16),
            [vmem((BLOCK, a), BF16) for a, _ in SETS],
            [vmem((NZ, 32, b), BF16) for _, b in SETS],
            [vmem((2, 16, wide), F32) for wide in parts],
            [vmem((2, 16, wide), BF16) for wide in parts],
            [vmem((16, wide), BF16) for wide in parts],
            [vmem((*long, 64, a), BF16) for a, _ in SETS],
            [vmem((*short, 16, a), BF16) for a, _ in SETS],
            [vmem((NZ, *short, 16, b), BF16) for _, b in SETS],
            [vmem((*long, 16, b), BF16) for _, b in SETS],
            dma((NZ + 2,)),
            dma((model // 256,)),
            dma((3, NZ)),
            dma((4, NZ)),
            *per_set(long), *per_set(short), *per_set((NZ, *short)), *per_set(long),
            *per_set(short), *per_set((4, *long)), *per_set(long), *per_set((NZ, *short)),
            dma((8,)),
            dma((8,)),
        ],
        compiler_params=pltpu.CompilerParams(
            collective_id=0, has_side_effects=True, vmem_limit_bytes=60 * 1024 * 1024
        ),
    )(active, resid, enc, enc_bias, dec, dec_bias, target)


def local(resid, enc_weight, enc_bias, active, dec_weight, dec_bias, target):
    layers, width, model = dec_weight.shape[1:]
    error, grads = step(
        active[0].T, resid[0], enc_weight[0], enc_bias,
        dec_weight[0].reshape(layers * width, model), dec_bias, target[0],
    )
    return error[None], grads.reshape(1, layers, width, model)


def solution(mesh):
    in_specs = (
        P("pair", None, None),
        P("pair", None, "feat"),
        P("pair", "feat"),
        P("pair", None, None),
        P("pair", None, "feat", None),
        P("pair", None),
        P("pair", "feat", None),
    )
    out_specs = (P("pair", "feat", None), P("pair", None, "feat", None))
    return jax.shard_map(local, mesh=mesh, in_specs=in_specs, out_specs=out_specs, check_vma=False)
```

time: 628 us -> 101 us (0.16)
  waiting for transfers between devices: 550 us -> 0 us
  Pallas kernels: 0 us -> 93.9 us
  matrix products: 42.1 us -> 0 us
  between operations: 13.8 us -> 0.64 us
  other arithmetic: 13.1 us -> 0 us
    reduce_scatter x1 -> x0, waiting for transfers between devices: 394 us -> none  [local(): lax.psum_scatter(lax.fori_loop(0, pair_index + 1, add_source, jnp.zeros((...]
    all_gather x2 -> x0, waiting for transfers between devices: 156 us -> none  [the longest x1 123 us: local(): lax.all_gather(error_shard.astype(jnp.bfloat16), 'feat', axis=0, tiled=True)]
    pallas_call x0 -> x1, Pallas kernels: none -> 93.9 us  [step(): pl.pallas_call(step_kernel, out_shape=(jax.ShapeDtypeStruct(target.shape,...]
    dot_general x7 -> x0, matrix products: 42.1 us -> none  [the longest x3 24.6 us: add_source(): jnp.dot(left_rows, weight_rows, preferred_element_type=jnp.float32)]
    reduce_or x1 -> x0, other arithmetic: 11.5 us -> none  [local(): chosen = jnp.any(active[0][:, :, None] == columns[None, None, :], axis=1)]
    broadcast_in_dim x2 -> x0, local copies, waits for them, and re-layouts: 6.81 us -> none  [the longest x1 4.28 us: local(): jnp.zeros((shard_rows * lax.axis_size('feat'), model_width), jnp.float32)]
    unnamed x8 -> x2, local copies, waits for them, and re-layouts: 0.02 us -> 6.36 us
  transfers between devices with their start and end apart: 3 -> 0, of which waited for: 3 -> 0; matrix products, arithmetic and copies ran while one was open for 0% -> 0% of each run, Pallas kernels for 0% -> 0%
where the time goes in v3:
time: 101 us
  Pallas kernels  93.9 us (93%)
  local copies, waits for them, and re-layouts  6.36 us (6%)
    pallas_call x1, Pallas kernels, step(): pl.pallas_call(step_kernel, out_shape=(jax.ShapeDtypeStruct(target.shape,...  93.9 us
    unnamed x2, local copies, waits for them, and re-layouts  6.36 us

profile of v3, /device:TPU:8, one launch (start us, length us, event | category | flops | bytes accessed | tf_op | source)
XLA Modules:
  0.0 100.9 jit_solution(6645089270631128940)
XLA Ops:
  0.6 93.9 %shard_map.86 = (f32[16,2048]{1,0:T(8,128)}, bf16[1024,2048]{1,0:T(8,128)(2,1)}) custom-call(s32[64,1024]{1,0:T(8,128)} %bitcast.13, bf16[1024,2048]{1,0:T(8,128)(2,1)} %bitcast.9, bf16[2048,256]{1,0:T(8,128)(2,1)} %bitcast.12, f32[1,256]{1,0:T(1,128)} %enc_bias_ref.1, bf16[1024,2048]{1,0:T(8,128)(2,1)} %bitcast.10, f32[1,2048]{1,0:T(1,128)} %dec_bias_ref.1, ...), custom_call_target="tpu_custom_call" | custom-call | tf_op jit(solution)/shard_map/pallas_call | solution.py:579
  94.5 1.6 %copy.11 = f32[1,16,2048]{2,1,0:T(8,128)} copy(f32[1,16,2048]{2,1,0:T(8,128)} %bitcast.14) | data formatting | bytes 262144
  96.1 4.8 %copy.12 = bf16[1,4,256,2048]{3,2,1,0:T(8,128)(2,1)} copy(bf16[1,4,256,2048]{3,2,1,0:T(8,128)(2,1)} %bitcast.11) | data formatting | bytes 8388608

commit v4 on v3

--- a/solution.py
+++ b/solution.py
@@ -17,7 +17,7 @@
 DISTANCES = (4, 3, -3, 2, -2, 1, -1, 0)
 LONG, SHORT = ((UP, 0), (DN, 1)), ((UP, 1), (DN, 0))
 STREAMS = LONG + SHORT
-WIRE, LATENCY = 47e3, 1.9
+WIRE, LATENCY = 42e3, 3.5
 
 
 class Plan:
@@ -211,7 +211,7 @@
 
 def step_kernel(
     act_ref, resid_hbm, enc_hbm, enc_bias_ref, dec_hbm, dec_bias_ref, target_ref,
-    err_ref, grads_hbm,
+    err_ref, grads_hbm, turned_hbm, late_hbm,
     resid, enc, dec, cat, part, full, turned, grads,
     mid_a, mid_b, end, give, take, held_az, held_ax, held_bx, held_bz,
     load, store, pair_send, pair_recv,
@@ -346,7 +346,9 @@
             collect(ks)
         step = 512
 
-        @pl.loop(2 * c, 2 * c + 2)
+        first = sum(map(sum, SETS[:c])) // step
+
+        @pl.loop(first, first + sum(SETS[c]) // step)
         def _(i):
             cols = pl.ds(pl.multiple_of(i * step, step), step)
             rows = jnp.concatenate([cat[order[k]] for k in ks], axis=0)
@@ -354,7 +356,7 @@
             for n, k in enumerate(ks):
                 part[order[k], :, cols] = product[n * BLOCK : (n + 1) * BLOCK]
 
-    decoded = [{}, {}]
+    decoded = [{} for _ in SETS]
     before = ()
     for ks in GROUPS:
         name = ("v", ks)
@@ -366,10 +368,10 @@
         ]
         plan.add(lambda ks=ks: relay(ks), 0.1, needs=[name], sends=[(("r", ks), "core", 3000)], bias=200.0)
         last = ()
-        for c in range(2):
+        for c in range(len(SETS)):
             last = [
                 plan.add(
-                    lambda ks=ks, c=c: decode(ks, c), 0.35 + 0.3 * len(ks),
+                    lambda ks=ks, c=c: decode(ks, c), (0.35 + 0.3 * len(ks)) * sum(SETS[c]) / 1024,
                     after=last, needs=[("r", ks)] if c == 0 else [], bias=40.0 - 40.0 * c,
                 )
             ]
@@ -379,7 +381,7 @@
     def turn(k):
         turned[:, pl.ds(pl.multiple_of(order[k] * BLOCK, BLOCK), BLOCK)] = cat[order[k]].T
 
-    turns = [plan.add(lambda k=k: turn(k), 0.35, after=[decoded[1][k]]) for k in range(NZ)]
+    turns = [plan.add(lambda k=k: turn(k), 0.35, after=[decoded[-1][k]]) for k in range(NZ)]
 
     def rows16(index, half):
         return pl.ds(pl.multiple_of(index * 32 + half * 16, 16), 16)
@@ -492,7 +494,7 @@
                 block = full.at[z, rows_of(x, 0), cols]
                 block[...] = error.astype(BF16)
                 err_ref[:, at] = error
-                copy = over_y(4 + which, block, block)
+                copy = over_y(2 * len(SETS) + which, block, block)
                 copy.start()
                 y_copies.append(copy)
                 first.first(0)
@@ -505,7 +507,7 @@
 
             def greet(which=which, cols=cols, first=first, ring=then[0]):
                 block = full.at[z, rows_of(x, 1), cols]
-                over_y(4 + which, block, block).wait_recv()
+                over_y(2 * len(SETS) + which, block, block).wait_recv()
                 first.first(1)
                 ring.first(1)
 
@@ -523,24 +525,37 @@
             arrived[which] = (at, ends)
 
     step = 256
-    grad_copies = []
-    for n in range(part.shape[2] // step):
+    early = sum(SETS[0])
+    copies_out = []
+
+    def put(src, dst):
+        copy = pltpu.make_async_copy(src, dst, store.at[len(copies_out)])
+        copy.start()
+        copies_out.append(copy)
+
+    plan.add(lambda: put(turned, turned_hbm), 0.05, after=turns)
+    for n in range(early // step):
 
         def grad(n=n):
             cols = slice(n * step, (n + 1) * step)
             rows = full[:, :, cols].reshape(-1, step)
             grads[:, cols] = jnp.dot(turned[...], rows, preferred_element_type=F32).astype(BF16)
-            copy = pltpu.make_async_copy(
-                grads.at[:, pl.ds(n * step, step)], grads_hbm.at[:, pl.ds(n * step, step)], store.at[n]
-            )
-            copy.start()
-            grad_copies.append(copy)
+            put(grads.at[:, pl.ds(n * step, step)], grads_hbm.at[:, pl.ds(n * step, step)])
 
         after = [*turns]
         for at, ends in arrived.values():
             if at.start < (n + 1) * step and at.stop > n * step:
                 after += ends
         plan.add(grad, 0.75, after=after)
+    for at, ends in arrived.values():
+        if at.start >= early:
+            wide = at.stop - at.start
+            plan.add(
+                lambda at=at, wide=wide: put(
+                    full.at[:, :, pl.ds(at.start, wide)], late_hbm.at[:, :, pl.ds(at.start - early, wide)]
+                ),
+                0.05, after=ends,
+            )
 
     plan.run()
 
@@ -564,7 +579,7 @@
         for k in range(NZ):
             send_piece(2, relayed, k, core_mate).wait_send()
 
-    for copy in grad_copies:
+    for copy in copies_out:
         copy.wait()
 
 
@@ -580,10 +595,12 @@
         step_kernel,
         out_shape=(
             jax.ShapeDtypeStruct(target.shape, F32),
-            jax.ShapeDtypeStruct((stacked, model), BF16),
+            jax.ShapeDtypeStruct((stacked, sum(SETS[0])), BF16),
+            jax.ShapeDtypeStruct((stacked, tokens), BF16),
+            jax.ShapeDtypeStruct((NZ, BLOCK, model - sum(SETS[0])), BF16),
         ),
         in_specs=[here, there, there, here, there, here, here],
-        out_specs=(here, there),
+        out_specs=(here, there, there, there),
         scratch_shapes=[
             vmem((NZ, BLOCK, model), BF16),
             vmem((model, width), BF16),
@@ -592,7 +609,7 @@
             vmem((NZ, BLOCK, model), BF16),
             vmem((NZ, BLOCK, model), BF16),
             vmem((stacked, tokens), BF16),
-            vmem((stacked, model), BF16),
+            vmem((stacked, sum(SETS[0])), BF16),
             [vmem((BLOCK, a), BF16) for a, _ in SETS],
             [vmem((NZ, 32, b), BF16) for _, b in SETS],
             [vmem((2, 16, wide), F32) for wide in parts],
@@ -603,13 +620,13 @@
             [vmem((NZ, *short, 16, b), BF16) for _, b in SETS],
             [vmem((*long, 16, b), BF16) for _, b in SETS],
             dma((NZ + 2,)),
-            dma((model // 256,)),
+            dma((sum(SETS[0]) // 256 + 3,)),
             dma((3, NZ)),
             dma((4, NZ)),
             *per_set(long), *per_set(short), *per_set((NZ, *short)), *per_set(long),
             *per_set(short), *per_set((4, *long)), *per_set(long), *per_set((NZ, *short)),
-            dma((8,)),
-            dma((8,)),
+            dma((4 * len(SETS),)),
+            dma((4 * len(SETS),)),
         ],
         compiler_params=pltpu.CompilerParams(
             collective_id=0, has_side_effects=True, vmem_limit_bytes=60 * 1024 * 1024
@@ -617,13 +634,58 @@
     )(active, resid, enc, enc_bias, dec, dec_bias, target)
 
 
+def finish_kernel(turned_ref, late_ref, early_ref, err_ref, out_ref, err_out_ref):
+    block = pl.program_id(0)
+
+    @pl.when(block == 0)
+    def _():
+        err_out_ref[...] = err_ref[...]
+
+    @pl.when(block < 2)
+    def _():
+        product = jnp.dot(turned_ref[...], late_ref[...], preferred_element_type=F32)
+        out_ref[...] = product.astype(BF16).reshape(out_ref.shape)
+
+    @pl.when(block >= 2)
+    def _():
+        out_ref[...] = early_ref[...].reshape(out_ref.shape)
+
+
+def finish(turned, late, early, error, layers):
+    stacked, tokens = turned.shape
+    block = 512
+    model = late.shape[1] + early.shape[1]
+    whole = lambda shape: pl.BlockSpec(shape, lambda i: (0, 0))
+    return pl.pallas_call(
+        finish_kernel,
+        grid=(model // block,),
+        out_shape=(
+            jax.ShapeDtypeStruct((layers, stacked // layers, model), BF16),
+            jax.ShapeDtypeStruct(error.shape, F32),
+        ),
+        in_specs=[
+            whole((stacked, tokens)),
+            pl.BlockSpec((tokens, block), lambda i: (0, jnp.minimum(i, 1))),
+            pl.BlockSpec((stacked, block), lambda i: (0, jnp.maximum(i - 2, 0))),
+            whole(error.shape),
+        ],
+        out_specs=(
+            pl.BlockSpec((layers, stacked // layers, block), lambda i: (0, 0, lax.rem(i + 2, 4))),
+            whole(error.shape),
+        ),
+        compiler_params=pltpu.CompilerParams(vmem_limit_bytes=60 * 1024 * 1024),
+    )(turned, late, early, error)
+
+
 def local(resid, enc_weight, enc_bias, active, dec_weight, dec_bias, target):
     layers, width, model = dec_weight.shape[1:]
-    error, grads = step(
+    tokens = resid.shape[1]
+    error, early, turned, late = step(
         active[0].T, resid[0], enc_weight[0], enc_bias,
         dec_weight[0].reshape(layers * width, model), dec_bias, target[0],
     )
-    return error[None], grads.reshape(1, layers, width, model)
+    grads, error = finish(turned, late.reshape(tokens, -1), early, error, layers)
+    return error[None], grads[None]
 
 
 def solution(mesh):

time: 101 us -> 98.2 us (0.972)
  local copies, waits for them, and re-layouts: 6.36 us -> 0 us
  Pallas kernels: 93.9 us -> 97.4 us
    pallas_call x0 -> x1, Pallas kernels: none -> 7.91 us  [finish(): pl.pallas_call(finish_kernel, grid=(model // block,), out_shape=(jax.Shap...]
    unnamed x2 -> x0, local copies, waits for them, and re-layouts: 6.36 us -> none
    pallas_call x1, Pallas kernels: 93.9 us -> 89.5 us  [step(): pl.pallas_call(step_kernel, out_shape=(jax.ShapeDtypeStruct(target.shape,...]
where the time goes in v4:
time: 98.2 us; the launch traced here: 98.1 us
  Pallas kernels  97.4 us (99%)
    pallas_call x1, Pallas kernels, step(): pl.pallas_call(step_kernel, out_shape=(jax.ShapeDtypeStruct(target.shape,...  89.5 us
    pallas_call x1, Pallas kernels, finish(): pl.pallas_call(finish_kernel, grid=(model // block,), out_shape=(jax.Shap...  7.91 us

profile of v4, /device:TPU:8, one launch (start us, length us, event | category | flops | bytes accessed | tf_op | source)
XLA Modules:
  0.0 98.1 jit_solution(15845381280449979724)
XLA Ops:
  0.6 89.5 %shard_map.86 = (f32[16,2048]{1,0:T(8,128)}, bf16[1024,1024]{1,0:T(8,128)(2,1)}, bf16[1024,1024]{1,0:T(8,128)(2,1)}, bf16[8,128,1024]{2,1,0:T(8,128)(2,1)}) custom-call(s32[64,1024]{1,0:T(8,128)} %bitcast.14, bf16[1024,2048]{1,0:T(8,128)(2,1)} %bitcast.10, bf16[2048,256]{1,0:T(8,128)(2,1)} %bitcast.13, f32[1,256]{1,0:T(1,128)} %enc_bias_ref.1, ...), custom_call_target="tpu_custom_call" | custom-call | tf_op jit(solution)/shard_map/pallas_call | solution.py:594
  90.1 7.9 %shard_map.87 = (bf16[4,256,2048]{2,1,0:T(8,128)(2,1)}, f32[16,2048]{1,0:T(8,128)}) custom-call(bf16[1024,1024]{1,0:T(8,128)(2,1)} %get-tuple-element.8.turned_ref, bf16[1024,1024]{1,0:T(8,128)(2,1)} %bitcast.12, bf16[1024,1024]{1,0:T(8,128)(2,1)} %get-tuple-element.10.early_ref, f32[16,2048]{1,0:T(8,128)} %get-tuple-element.11.err_ref), custom_call_target="tpu_custom_call" | custom-call | tf_op jit(solution)/shard_map/pallas_call | solution.py:659

commit v5 on v4

--- a/solution.py
+++ b/solution.py
@@ -17,7 +17,7 @@
 DISTANCES = (4, 3, -3, 2, -2, 1, -1, 0)
 LONG, SHORT = ((UP, 0), (DN, 1)), ((UP, 1), (DN, 0))
 STREAMS = LONG + SHORT
-WIRE, LATENCY = 42e3, 3.5
+WIRE, LATENCY = 42e3, 2.6
 
 
 class Plan:
@@ -634,28 +634,41 @@
     )(active, resid, enc, enc_bias, dec, dec_bias, target)
 
 
-def finish_kernel(turned_ref, late_ref, early_ref, err_ref, out_ref, err_out_ref):
-    block = pl.program_id(0)
+def finish_kernel(turned_hbm, late_hbm, early_ref, err_ref, out_ref, err_out_ref, turned, late, load):
+    block, step = pl.program_id(0), out_ref.shape[2]
+    copies = [pltpu.make_async_copy(turned_hbm, turned, load.at[0])]
+    for n in range(2):
+        cols = pl.ds(n * step, step)
+        copies.append(pltpu.make_async_copy(late_hbm.at[:, cols], late.at[:, cols], load.at[1 + n]))
 
     @pl.when(block == 0)
     def _():
+        for copy in copies:
+            copy.start()
         err_out_ref[...] = err_ref[...]
 
     @pl.when(block < 2)
     def _():
-        product = jnp.dot(turned_ref[...], late_ref[...], preferred_element_type=F32)
-        out_ref[...] = product.astype(BF16).reshape(out_ref.shape)
-
-    @pl.when(block >= 2)
-    def _():
         out_ref[...] = early_ref[...].reshape(out_ref.shape)
+
+    for n in range(2):
+
+        @pl.when(block == 2 + n)
+        def _():
+            if n == 0:
+                copies[0].wait()
+            copies[1 + n].wait()
+            rows = late[:, n * step : (n + 1) * step]
+            product = jnp.dot(turned[...], rows, preferred_element_type=F32)
+            out_ref[...] = product.astype(BF16).reshape(out_ref.shape)
 
 
 def finish(turned, late, early, error, layers):
     stacked, tokens = turned.shape
     block = 512
     model = late.shape[1] + early.shape[1]
-    whole = lambda shape: pl.BlockSpec(shape, lambda i: (0, 0))
+    there = pl.BlockSpec(memory_space=pl.ANY)
+    whole = pl.BlockSpec(error.shape, lambda i: (0, 0))
     return pl.pallas_call(
         finish_kernel,
         grid=(model // block,),
@@ -664,15 +677,20 @@
             jax.ShapeDtypeStruct(error.shape, F32),
         ),
         in_specs=[
-            whole((stacked, tokens)),
-            pl.BlockSpec((tokens, block), lambda i: (0, jnp.minimum(i, 1))),
-            pl.BlockSpec((stacked, block), lambda i: (0, jnp.maximum(i - 2, 0))),
-            whole(error.shape),
+            there,
+            there,
+            pl.BlockSpec((stacked, block), lambda i: (0, jnp.minimum(i, 1))),
+            whole,
         ],
         out_specs=(
-            pl.BlockSpec((layers, stacked // layers, block), lambda i: (0, 0, lax.rem(i + 2, 4))),
-            whole(error.shape),
+            pl.BlockSpec((layers, stacked // layers, block), lambda i: (0, 0, i)),
+            whole,
         ),
+        scratch_shapes=[
+            pltpu.VMEM((stacked, tokens), BF16),
+            pltpu.VMEM(late.shape, BF16),
+            pltpu.SemaphoreType.DMA((3,)),
+        ],
         compiler_params=pltpu.CompilerParams(vmem_limit_bytes=60 * 1024 * 1024),
     )(turned, late, early, error)
 

time: 98.2 us -> 97.5 us (level)
  no operation moved by 1% of the time
where the time goes in v5:
time: 97.5 us; the launch traced here: 97.3 us
  Pallas kernels  96.5 us (99%)
    pallas_call x1, Pallas kernels, step(): pl.pallas_call(step_kernel, out_shape=(jax.ShapeDtypeStruct(target.shape,...  89 us
    pallas_call x1, Pallas kernels, finish(): pl.pallas_call(finish_kernel, grid=(model // block,), out_shape=(jax.Shap...  7.52 us

profile of v5, /device:TPU:8, one launch (start us, length us, event | category | flops | bytes accessed | tf_op | source)
XLA Modules:
  0.0 97.3 jit_solution(8017758065299934694)
XLA Ops:
  0.6 89.0 %shard_map.86 = (f32[16,2048]{1,0:T(8,128)}, bf16[1024,1024]{1,0:T(8,128)(2,1)}, bf16[1024,1024]{1,0:T(8,128)(2,1)}, bf16[8,128,1024]{2,1,0:T(8,128)(2,1)}) custom-call(s32[64,1024]{1,0:T(8,128)} %bitcast.14, bf16[1024,2048]{1,0:T(8,128)(2,1)} %bitcast.10, bf16[2048,256]{1,0:T(8,128)(2,1)} %bitcast.13, f32[1,256]{1,0:T(1,128)} %enc_bias_ref.1, ...), custom_call_target="tpu_custom_call" | custom-call | tf_op jit(solution)/shard_map/pallas_call | solution.py:594
  89.7 7.5 %shard_map.87 = (bf16[4,256,2048]{2,1,0:T(8,128)(2,1)}, f32[16,2048]{1,0:T(8,128)}) custom-call(bf16[1024,1024]{1,0:T(8,128)(2,1)} %get-tuple-element.8.turned_hbm, bf16[1024,1024]{1,0:T(8,128)(2,1)} %bitcast.12, bf16[1024,1024]{1,0:T(8,128)(2,1)} %get-tuple-element.10.early_ref, f32[16,2048]{1,0:T(8,128)} %get-tuple-element.11.err_ref), custom_call_target="tpu_custom_call" | custom-call | tf_op jit(solution)/shard_map/pallas_call | solution.py:672
